TPU v7x, 256 devices: a whole 4x4x8 slice. The times are simulated.
256 devices in a mesh: freq: 32 (over y, z), tcol: 4 (over x), trow: 2 (over core).
Axes of the slice: x: 4, y: 4, z: 8, core: 2. Of those that a mesh axis runs over, the one named last changes fastest.
Arguments:
- focal_field: bfloat16 [128, 6144, 256], P('freq', ('tcol', 'trow')), may hold values from -6 to 6
- mute_window: int32 [128, 6144], P('freq', ('tcol', 'trow')), may hold values from 64 to 255
- tile_ranks: int32 [32, 16, 16], P('freq', None, ('tcol', 'trow')), may hold values from 32 to 96
- left_factors: bfloat16 [32, 16, 16, 96, 2, 384], P('freq', ('tcol', 'trow')), may hold values from -0.15625 to 0.15625
- right_factors: bfloat16 [32, 16, 16, 96, 2, 384], P('freq', None, ('tcol', 'trow')), may hold values from -0.3125 to 0.3125
Outputs:
- first_pass: bfloat16 [128, 6144, 256], P('freq', ('tcol', 'trow'))
- second_pass: bfloat16 [128, 6144, 256], P('freq', ('tcol', 'trow'))
Inputs may be any that keep to these rules, and one draw needn't show every extreme that they name: `mute_window`: samples at times below this index are kept, the others set to zero. Only the first tile_ranks components of a tile's factors enter the operator.
All inputs are finite; a program needn't handle non-finite values.
Results may differ from a plain program's by a relative error of at most 0.013.
Values may be sent and summed in bfloat16 or wider, within the bound.
No kernel may reach another device: no remote copies, remote signals or barrier semaphores. Data moves between devices by JAX's collectives and lax.ppermute only.
A program may use at most 64 MiB of HBM per device.

v0:
```python
import math

import jax
import jax.numpy as jnp
from jax import lax
from jax.sharding import PartitionSpec as P


def spectral_table(count_freq, time_len):
    bins = jnp.arange(1, count_freq + 1, dtype=jnp.int32)
    times = jnp.arange(time_len, dtype=jnp.int32)
    turns = bins[:, None] * times[None, :] % time_len
    phase = turns.astype(jnp.float32) * (2.0 * math.pi / time_len)
    return jnp.stack([jnp.cos(phase), -jnp.sin(phase)]).astype(jnp.bfloat16)


def body(focal_field, mute_window, tile_ranks, left_factors, right_factors):
    focal_dev, src_rows, time_len = focal_field.shape
    freq_dev, row_tiles, all_tiles, rank_cap, parts_two, tile_len = left_factors.shape
    col_tiles = right_factors.shape[2]
    spectral = spectral_table(freq_dev * lax.axis_size("freq"), time_len)
    keep_time = lax.broadcasted_iota(jnp.int32, focal_field.shape, 2) < mute_window[:, :, None]
    used_rank = (
        lax.broadcasted_iota(jnp.int32, (freq_dev, all_tiles, col_tiles, rank_cap), 3)
        < tile_ranks[:, :, :, None]
    )
    signal = jnp.where(keep_time, focal_field, jnp.zeros_like(focal_field))
    outputs = []
    for conj_sign in (1.0, -1.0):
        spectrum = jnp.einsum("dft,pst->dfps", spectral, signal, preferred_element_type=jnp.float32)
        spectrum = (spectrum * (1.0 / math.sqrt(time_len))).astype(jnp.bfloat16)
        local_spec = lax.all_to_all(spectrum, "freq", split_axis=1, concat_axis=2, tiled=True)
        all_points = local_spec.shape[2]
        local_spec = local_spec.reshape(2, freq_dev, all_points, col_tiles, tile_len)
        products = jnp.einsum(
            "fijkcl,dfpjl->fijkcdp", right_factors, local_spec, preferred_element_type=jnp.float32
        )
        real_part = products[:, :, :, :, 0, 0] + conj_sign * products[:, :, :, :, 1, 1]
        imag_part = products[:, :, :, :, 0, 1] - conj_sign * products[:, :, :, :, 1, 0]
        stacked = jnp.stack([real_part, imag_part], axis=4)
        coefficients = jnp.where(
            used_rank[:, :, :, :, None, None], stacked, jnp.zeros_like(stacked)
        )
        coefficients = coefficients.astype(jnp.bfloat16).reshape(
            freq_dev, all_tiles, col_tiles, rank_cap, 2 * all_points
        )
        direct = coefficients.reshape(
            freq_dev, all_tiles // row_tiles, row_tiles, 1, col_tiles, rank_cap, 2 * all_points
        )
        direct = lax.all_to_all(direct, ("tcol", "trow"), split_axis=1, concat_axis=3, tiled=True)
        gathered = direct.reshape(freq_dev, row_tiles, all_tiles, rank_cap, 2, all_points)
        outer_prod = jnp.einsum(
            "fijkcl,fijkdp->cdfpil", left_factors, gathered, preferred_element_type=jnp.float32
        )
        reply_real = outer_prod[0, 0] - conj_sign * outer_prod[1, 1]
        reply_imag = outer_prod[0, 1] + conj_sign * outer_prod[1, 0]
        replies = jnp.stack([reply_real, reply_imag]).reshape(
            2, freq_dev, all_points, row_tiles * tile_len
        )
        replies = replies.astype(jnp.bfloat16)
        returned = lax.all_to_all(replies, "freq", split_axis=2, concat_axis=1, tiled=True)
        wave_field = jnp.einsum(
            "dfps,dft->pst", returned, spectral, preferred_element_type=jnp.float32
        )
        wave_field = wave_field * (2.0 / math.sqrt(time_len))
        signal = jnp.where(keep_time, wave_field, jnp.zeros_like(wave_field)).astype(jnp.bfloat16)
        outputs.append(signal)
    return (outputs[0], outputs[1])


def solution(mesh):
    in_specs = (
        P("freq", ("tcol", "trow"), None),
        P("freq", ("tcol", "trow")),
        P("freq", None, ("tcol", "trow")),
        P("freq", ("tcol", "trow"), None, None, None, None),
        P("freq", None, ("tcol", "trow"), None, None, None),
    )
    out_specs = (P("freq", ("tcol", "trow"), None), P("freq", ("tcol", "trow"), None))
    return jax.shard_map(body, mesh=mesh, in_specs=in_specs, out_specs=out_specs, check_vma=False)
```

profile of v0, /device:TPU:32, one launch (start us, length us, event | category | flops | bytes accessed | tf_op | source)
XLA Modules:
  0.0 176.0 jit_solution(306989996540478033)
XLA Ops:
  0.9 2.1 %fusion.55 = bf16[2,32,4,768]{3,1,2,0:T(8,128)(2,1)S(1)} fusion(bf16[4,768,256]{2,1,0:T(8,128)(2,1)} %param.5, s32[4,768]{1,0:T(4,128)} %param.6, bf16[1,32,256]{2,1,0:T(8,128)(2,1)S(1)} %get-tuple-element.7, bf16[1,32,256]{2,1,0:T(8,128)(2,1)S(1)} %get-tuple-element.6), kind=kOutput, calls=%fused_computation.49 | convolution fusion | flops 102694912 | bytes 2011136 | tf_op jit(solution)/shard_map/dft,pst->dfps/dot_general | solution.py:30
  3.0 1.1 copy.106
  4.0 11.4 %all-to-all-start = ((bf16[2,32,4,768]{3,2,0,1:T(4,128)(2,1)}), bf16[2,32,4,768]{3,2,0,1:T(4,128)(2,1)S(1)}, u32[]{:S(2)}, u32[]{:S(2)}) async-start(bf16[2,32,4,768]{3,2,0,1:T(4,128)(2,1)} %copy.106), calls=%async_computation | async-start | bytes 786432 | tf_op jit(solution)/shard_map/all_to_all | solution.py:32
  15.6 14.7 %all-to-all-done = bf16[2,32,4,768]{3,2,0,1:T(4,128)(2,1)S(1)} async-done(((bf16[2,32,4,768]{3,2,0,1:T(4,128)(2,1)}), bf16[2,32,4,768]{3,2,0,1:T(4,128)(2,1)S(1)}, u32[]{:S(2)}, u32[]{:S(2)}) %all-to-all-start) | async-done | bytes 393248 | tf_op jit(solution)/shard_map/all_to_all | solution.py:32
  30.6 3.7 %fusion.15 = f32[1,16,2,96,2,2,128]{6,3,4,1,5,2,0:T(8,128)S(1)} fusion(bf16[16,2,96,2,384,1]{4,3,2,1,0,5:T(2,128)(2,1)} %bitcast.126, bf16[2,128,2,384,1,1]{3,2,1,0,5,4:T(2,128)(2,1)S(1)} %bitcast.132), kind=kOutput, calls=%fused_computation.22 | convolution fusion | flops 1207959552 | bytes 11403264 | tf_op jit(solution)/shard_map/fijkcl,dfpjl->fijkcdp/dot_general | solution.py:35
  34.9 2.5 %copy.112 = f32[1,16,2,96,2,128]{5,4,0,3,2,1:T(2,128)S(1)} copy(f32[1,16,2,96,2,128]{5,3,1,2,4,0:T(8,128)S(1)} %pad_maximum_fusion) | data formatting | bytes 6291456 | tf_op jit(solution)/shard_map/stack | solution.py:40
  37.4 4.7 %fusion.8 = bf16[1,8,2,1,2,96,256]{6,0,5,4,2,1,3:T(2,128)(2,1)S(1)} fusion(f32[1,8,2,1,2,96,256]{6,0,5,4,2,1,3:T(1,128)S(1)} %bitcast.129, pred[8,2,2,96]{3,2,1,0:T(4,128)(4,1)S(1)} %iota_compare_fusion.1), kind=kLoop, calls=%fused_computation.10 | loop fusion | flops 786432 | bytes 4721664 | tf_op jit(solution)/shard_map/convert_element_type | solution.py:44
  42.5 25.7 %all_to_all.72 = bf16[1,8,2,1,2,96,256]{6,5,4,3,2,0,1:T(8,128)(2,1)S(1)} all-to-all(bf16[1,8,2,1,2,96,256]{6,5,4,3,2,0,1:T(8,128)(2,1)S(1)} %copy.113), channel_id=1, replica_groups=mesh['freq'=32,'tcol'=4,'trow'=2] {'tcol','trow'}, dimensions={1} | all-to-all | bytes 3145728 | tf_op jit(solution)/shard_map/all_to_all | solution.py:50
  68.3 0.4 reshape.546
  68.7 3.8 %fusion.36 = f32[2,2,1,128,2,384]{5,3,0,1,4,2:T(8,128)S(1)} fusion(bf16[2,16,96,2,384,1]{4,3,2,1,0,5:T(2,128)(2,1)} %bitcast.143, bf16[2,16,96,2,128,1]{4,3,2,1,0,5:T(2,128)(2,1)S(1)} %bitcast.134), kind=kOutput, calls=%fused_computation.44 | convolution fusion | flops 1207959552 | bytes 7864320 | tf_op jit(solution)/shard_map/fijkcl,fijkdp->cdfpil/dot_general | solution.py:52
  73.1 0.4 copy.119
  73.5 19.2 %all_to_all.73 = bf16[2,1,128,768]{3,0,1,2:T(2,128)(2,1)S(1)} all-to-all(bf16[2,1,128,768]{3,0,1,2:T(2,128)(2,1)S(1)} %copy.119), channel_id=1, replica_groups=mesh['freq'=32,'tcol'=4,'trow'=2] {'freq'}, dimensions={2} | all-to-all | bytes 786432 | tf_op jit(solution)/shard_map/all_to_all | solution.py:61
  92.7 0.9 fusion.13
  93.7 0.6 fusion.52
  94.6 18.5 %all_to_all.74 = bf16[2,32,4,768]{3,2,0,1:T(4,128)(2,1)S(1)} all-to-all(bf16[2,32,4,768]{3,2,0,1:T(4,128)(2,1)S(1)} %copy.121), channel_id=1, replica_groups=mesh['freq'=32,'tcol'=4,'trow'=2] {'freq'}, dimensions={1} | all-to-all | bytes 786432 | tf_op jit(solution)/shard_map/all_to_all | solution.py:32
  113.4 3.7 %fusion.18 = f32[1,16,2,96,2,2,128]{6,3,4,1,5,2,0:T(8,128)S(1)} fusion(bf16[16,2,96,2,384,1]{4,3,2,1,0,5:T(2,128)(2,1)} %bitcast.127, bf16[2,128,2,384,1,1]{3,2,1,0,5,4:T(2,128)(2,1)S(1)} %bitcast.133), kind=kOutput, calls=%fused_computation.23 | convolution fusion | flops 1207959552 | bytes 11403264 | tf_op jit(solution)/shard_map/fijkcl,dfpjl->fijkcdp/dot_general | solution.py:35
  117.9 2.5 %copy.128 = f32[1,16,2,96,2,128]{5,4,0,3,2,1:T(2,128)S(1)} copy(f32[1,16,2,96,2,128]{5,3,1,2,4,0:T(8,128)S(1)} %pad_maximum_fusion.1) | data formatting | bytes 6291456 | tf_op jit(solution)/shard_map/stack | solution.py:40
  120.4 4.7 %fusion.9 = bf16[1,8,2,1,2,96,256]{6,0,5,4,2,1,3:T(2,128)(2,1)S(1)} fusion(f32[1,8,2,1,2,96,256]{6,0,5,4,2,1,3:T(1,128)S(1)} %bitcast.128, pred[8,2,2,96]{3,2,1,0:T(4,128)(4,1)S(1)} %iota_compare_fusion.1), kind=kLoop, calls=%fused_computation.11 | loop fusion | flops 786432 | bytes 4721664 | tf_op jit(solution)/shard_map/convert_element_type | solution.py:44
  125.4 24.3 %all_to_all.75 = bf16[1,8,2,1,2,96,256]{6,5,4,3,2,0,1:T(8,128)(2,1)S(1)} all-to-all(bf16[1,8,2,1,2,96,256]{6,5,4,3,2,0,1:T(8,128)(2,1)S(1)} %copy.129), channel_id=1, replica_groups=mesh['freq'=32,'tcol'=4,'trow'=2] {'tcol','trow'}, dimensions={1} | all-to-all | bytes 3145728 | tf_op jit(solution)/shard_map/all_to_all | solution.py:50
  149.9 0.4 reshape.549
  150.3 3.8 %fusion.41 = f32[2,2,1,128,2,384]{5,3,0,1,4,2:T(8,128)S(1)} fusion(bf16[2,16,96,2,384,1]{4,3,2,1,0,5:T(2,128)(2,1)} %bitcast.144, bf16[2,16,96,2,128,1]{4,3,2,1,0,5:T(2,128)(2,1)S(1)} %bitcast.135), kind=kOutput, calls=%fused_computation.45 | convolution fusion | flops 1207959552 | bytes 7864320 | tf_op jit(solution)/shard_map/fijkcl,fijkdp->cdfpil/dot_general | solution.py:52
  154.6 0.4 copy.135
  155.1 19.1 %all_to_all.76 = bf16[2,1,128,768]{3,0,1,2:T(2,128)(2,1)S(1)} all-to-all(bf16[2,1,128,768]{3,0,1,2:T(2,128)(2,1)S(1)} %copy.135), channel_id=1, replica_groups=mesh['freq'=32,'tcol'=4,'trow'=2] {'freq'}, dimensions={2} | all-to-all | bytes 786432 | tf_op jit(solution)/shard_map/all_to_all | solution.py:61
  174.2 1.8 %fusion.11 = bf16[4,768,256]{2,1,0:T(8,128)(2,1)} fusion(s32[4,768]{1,0:T(4,128)S(1)} %copy-done.2, bf16[2,32,4,768]{3,0,2,1:T(2,128)(2,1)S(1)} %bitcast.140, bf16[1,32,256]{2,1,0:T(8,128)(2,1)S(1)} %get-tuple-element.7, bf16[1,32,256]{2,1,0:T(8,128)(2,1)S(1)} %get-tuple-element.6), kind=kOutput, calls=%fused_computation.16 | convolution fusion | flops 103825408 | bytes 2011136 | tf_op jit(solution)/shard_map/dfps,dft->pst/dot_general | solution.py:62
  (33 shorter events, 4.6 us)
Async XLA Ops:
  0.6 14.7 %copy-start.1 = (s32[1,16,2]{1,2,0:T(2,128)S(1)}, s32[1,16,2]{1,2,0:T(2,128)}, u32[]{:S(2)}) copy-start(s32[1,16,2]{1,2,0:T(2,128)} %param.7) | copy-start | bytes 388
  4.0 26.2 %all-to-all-start = ((bf16[2,32,4,768]{3,2,0,1:T(4,128)(2,1)}), bf16[2,32,4,768]{3,2,0,1:T(4,128)(2,1)S(1)}, u32[]{:S(2)}, u32[]{:S(2)}) async-start(bf16[2,32,4,768]{3,2,0,1:T(4,128)(2,1)} %copy.106), calls=%async_computation | async-start | bytes 786432 | tf_op jit(solution)/shard_map/all_to_all | solution.py:32
  72.6 20.1 %copy-start.2 = (s32[4,768]{1,0:T(4,128)S(1)}, s32[4,768]{1,0:T(4,128)}, u32[]{:S(2)}) copy-start(s32[4,768]{1,0:T(4,128)} %param.6) | copy-start | bytes 36868
  93.7 19.5 %copy-start = (bf16[4,768,256]{2,1,0:T(8,128)(2,1)}, bf16[4,768,256]{2,1,0:T(8,128)(2,1)S(1)}, u32[]{:S(2)}) copy-start(bf16[4,768,256]{2,1,0:T(8,128)(2,1)S(1)} %fusion.13) | copy-start | bytes 4718596
where the time goes:
time: 176 us
  blocking collectives  107 us (61%)
  matrix products  20.5 us (12%)
  waiting for transfers between devices  14.7 us (8%)
  starting transfers between devices  11.4 us (6%)
  other arithmetic  11.1 us (6%)
  local copies, waits for them, and re-layouts  10.5 us (6%)
    all_to_all x2, blocking collectives, body(): lax.all_to_all(direct, ('tcol', 'trow'), split_axis=1, concat_axis=3, til...  50 us
    all_to_all x2, blocking collectives, body(): lax.all_to_all(replies, 'freq', split_axis=2, concat_axis=1, tiled=True)  38.3 us
    all_to_all x1, blocking collectives, body(): lax.all_to_all(spectrum, 'freq', split_axis=1, concat_axis=2, tiled=True)  18.5 us
    all_to_all x1, waiting for transfers between devices, body(): lax.all_to_all(spectrum, 'freq', split_axis=1, concat_axis=2, tiled=True)  14.7 us
    all_to_all x1, starting transfers between devices, body(): lax.all_to_all(spectrum, 'freq', split_axis=1, concat_axis=2, tiled=True)  11.4 us
    convert_element_type x2, other arithmetic, body(): coefficients.astype(jnp.bfloat16)  9.32 us
    dot_general x2, matrix products, body(): jnp.einsum('fijkcl,fijkdp->cdfpil', left_factors, gathered, preferred_ele...  7.62 us
    dot_general x2, matrix products, body(): jnp.einsum('fijkcl,dfpjl->fijkcdp', right_factors, local_spec, preferred_...  7.49 us
  transfers between devices with their start and end apart: 1, of which 1 were waited for; matrix products, arithmetic and copies ran while one was open for 0% of the time, Pallas kernels for 0%

commit v1 on v0

v1 whole, which is shorter than its diff:
```python
import functools
import math

import jax
import jax.numpy as jnp
import numpy as np
from jax import lax
from jax.experimental import pallas as pl
from jax.experimental.pallas import tpu as pltpu
from jax.sharding import PartitionSpec as P

MIB = 1 << 20


def spectral_rows(count_freq, time_len, repeat):
    row = np.arange(count_freq * 2 * repeat)
    bins = row // (2 * repeat) + 1
    part = (row // repeat) % 2
    turns = bins[:, None] * np.arange(time_len)[None, :] % time_len
    phase = turns.astype(np.float32) * np.float32(2.0 * math.pi / time_len)
    table = np.where(part[:, None] == 0, np.cos(phase), -np.sin(phase))
    return jnp.asarray(table.astype(np.float32)).astype(jnp.bfloat16)


def nt_dot(a, b):
    return lax.dot_general(a, b, (((1,), (1,)), ((), ())), preferred_element_type=jnp.float32)


def tn_dot(a, b):
    return lax.dot_general(a, b, (((0,), (0,)), ((), ())), preferred_element_type=jnp.float32)


def swap_parts(x, half):
    rows, cols = x.shape
    grouped = x.reshape(rows // (2 * half), 2 * half, cols)
    return pltpu.roll(grouped, half, axis=1).reshape(rows, cols)


def part_sign(shape, half, sign):
    row = lax.broadcasted_iota(jnp.int32, shape, 0)
    return jnp.where(row % (2 * half) < half, sign, -sign).astype(jnp.float32)


def pick_point(table, point, points):
    row = lax.broadcasted_iota(jnp.int32, table.shape, 0)
    return jnp.where(row % points == point, table, jnp.zeros_like(table))


def to_freq(table, signals, scale):
    points = len(signals)
    total = None
    for point in range(points):
        part = nt_dot(pick_point(table, point, points), signals[point])
        total = part if total is None else total + part
    return (total * scale).astype(jnp.bfloat16)


def to_time(table, replies, window, scale, points):
    flipped = replies.T
    blocks = []
    for point in range(points):
        wave = jnp.dot(
            flipped, pick_point(table, point, points), preferred_element_type=jnp.float32
        ) * scale
        time_at = lax.broadcasted_iota(jnp.int32, wave.shape, 1)
        kept = time_at < window[:, point : point + 1]
        blocks.append(jnp.where(kept, wave, jnp.zeros_like(wave)).astype(jnp.bfloat16))
    return blocks


def stand_window(window):
    wide = window.astype(jnp.float32)
    padded = jnp.concatenate([wide, jnp.zeros((8 - wide.shape[0], wide.shape[1]), jnp.float32)])
    return padded.T.astype(jnp.int32)


def first_kernel(scale, table_ref, field_ref, window_ref, out_ref):
    points = field_ref.shape[0]
    signals = []
    window = stand_window(window_ref[...])
    for point in range(points):
        block = field_ref[point].astype(jnp.float32)
        time_at = lax.broadcasted_iota(jnp.int32, block.shape, 1)
        kept = time_at < window[:, point : point + 1]
        signals.append(jnp.where(kept, block, jnp.zeros_like(block)).astype(jnp.bfloat16))
    out_ref[...] = to_freq(table_ref[...], signals, scale)


def middle_kernel(back_scale, scale, table_ref, reply_ref, window_ref, pass_ref, out_ref):
    points = pass_ref.shape[0]
    table = table_ref[...]
    blocks = to_time(table, reply_ref[...], stand_window(window_ref[...]), back_scale, points)
    for point in range(points):
        pass_ref[point] = blocks[point]
    out_ref[...] = to_freq(table, blocks, scale)


def last_kernel(back_scale, table_ref, reply_ref, window_ref, pass_ref):
    points = pass_ref.shape[0]
    blocks = to_time(table_ref[...], reply_ref[...], stand_window(window_ref[...]), back_scale, points)
    for point in range(points):
        pass_ref[point] = blocks[point]


def right_kernel(rank_ref, factor_ref, out_ref):
    _, all_tiles, col_tiles, rank_cap, parts, tile_len = factor_ref.shape
    block = 16

    def one_tile(number, carry):
        tile, col = number // col_tiles, number % col_tiles
        rank = rank_ref[tile, col]
        for start in range(0, rank_cap, block):
            rows = pl.ds(pl.multiple_of(tile * rank_cap + start, block), block)

            @pl.when(start < rank)
            def _():
                part = factor_ref[0, tile, col, start : start + block]
                part = part.reshape(block, parts * tile_len)
                row = lax.broadcasted_iota(jnp.int32, part.shape, 0) + start
                out_ref[col, rows] = jnp.where(row < rank, part, jnp.zeros_like(part))

            @pl.when(start >= rank)
            def _():
                out_ref[col, rows] = jnp.zeros((block, parts * tile_len), out_ref.dtype)

        return carry

    lax.fori_loop(0, all_tiles * col_tiles, one_tile, 0)


def left_kernel(factor_ref, out_ref):
    _, row_tiles, all_tiles, rank_cap, parts, tile_len = factor_ref.shape

    def one_tile(number, carry):
        tile, col = number // all_tiles, number % all_tiles
        part = factor_ref[0, tile, col].reshape(rank_cap, parts * tile_len)
        out_ref[tile, pl.ds(pl.multiple_of(col * rank_cap, 16), rank_cap)] = part
        return carry

    lax.fori_loop(0, row_tiles * all_tiles, one_tile, 0)


def coef_kernel(sign, half, spec_ref, right_ref, out_ref):
    all_tiles, col_tiles, rank_cap, rows = out_ref.shape
    tile_len = spec_ref.shape[1] // col_tiles
    for col in range(col_tiles):
        block = spec_ref[:, col * tile_len : (col + 1) * tile_len]
        wide = block.astype(jnp.float32)
        other = swap_parts(wide, half) * part_sign(wide.shape, half, sign)
        paired = jnp.concatenate([block, other.astype(jnp.bfloat16)], axis=1)
        coef = nt_dot(right_ref[col], paired).astype(jnp.bfloat16)
        for tile in range(all_tiles):
            out_ref[tile, col] = coef[tile * rank_cap : (tile + 1) * rank_cap]


def reply_kernel(sign, half, coef_ref, left_ref, out_ref):
    sources, row_tiles, depth, rows = coef_ref.shape
    tile_len = out_ref.shape[1] // row_tiles
    for tile in range(row_tiles):
        coef = coef_ref[:, tile].reshape(sources * depth, rows)
        both = tn_dot(coef, left_ref[tile])
        other = both[:, tile_len:]
        other = swap_parts(other, half) * part_sign(other.shape, half, -sign)
        reply = both[:, :tile_len] + other
        out_ref[:, tile * tile_len : (tile + 1) * tile_len] = reply.astype(jnp.bfloat16)


def body(focal_field, mute_window, tile_ranks, left_factors, right_factors):
    points, src_rows, time_len = focal_field.shape
    _, row_tiles, all_tiles, rank_cap, parts_two, tile_len = left_factors.shape
    col_tiles = right_factors.shape[2]
    freqs = lax.axis_size("freq")
    groups = all_tiles // row_tiles
    rows = freqs * 2 * points
    table = spectral_rows(freqs, time_len, points)
    window = mute_window
    scale = 1.0 / math.sqrt(time_len)
    back_scale = 2.0 / math.sqrt(time_len)
    step = 256
    chunks = src_rows // step
    bf16 = jnp.bfloat16

    whole = pl.BlockSpec(memory_space=pltpu.VMEM)
    table_spec = pl.BlockSpec((rows, time_len), lambda s: (0, 0))
    field_spec = pl.BlockSpec((points, step, time_len), lambda s: (0, s, 0))
    window_spec = pl.BlockSpec((points, step), lambda s: (0, s))
    rows_spec = pl.BlockSpec((rows, step), lambda s: (0, s))
    params = pltpu.CompilerParams(vmem_limit_bytes=24 * MIB)
    rows_shape = jax.ShapeDtypeStruct((rows, src_rows), bf16)
    pass_shape = jax.ShapeDtypeStruct(focal_field.shape, bf16)

    smem = pl.BlockSpec(memory_space=pltpu.SMEM)
    with jax.named_scope("prep_right"):
        right = pl.pallas_call(
            right_kernel,
            in_specs=[smem, whole],
            out_specs=whole,
            out_shape=jax.ShapeDtypeStruct(
                (col_tiles, all_tiles * rank_cap, parts_two * tile_len), bf16
            ),
            compiler_params=params,
            name="prep_right",
        )(tile_ranks.reshape(all_tiles, col_tiles), right_factors)
    with jax.named_scope("prep_left"):
        left = pl.pallas_call(
            left_kernel,
            in_specs=[whole],
            out_specs=whole,
            out_shape=jax.ShapeDtypeStruct(
                (row_tiles, all_tiles * rank_cap, parts_two * tile_len), bf16
            ),
            compiler_params=params,
            name="prep_left",
        )(left_factors)

    with jax.named_scope("dft_first"):
        spectrum = pl.pallas_call(
            functools.partial(first_kernel, scale),
            grid=(chunks,),
            in_specs=[table_spec, field_spec, window_spec],
            out_specs=rows_spec,
            out_shape=rows_shape,
            compiler_params=pltpu.CompilerParams(vmem_limit_bytes=58 * MIB),
            name="dft_first",
        )(table, focal_field, window)

    outputs = []
    for number, sign in enumerate((1.0, -1.0)):
        with jax.named_scope(f"to_freq{number}"):
            moved = lax.all_to_all(
                spectrum.reshape(freqs, 2 * points, src_rows), "freq",
                split_axis=0, concat_axis=0, tiled=True,
            ).reshape(rows, src_rows)
        with jax.named_scope(f"coef{number}"):
            coef = pl.pallas_call(
                functools.partial(coef_kernel, sign, points),
                in_specs=[whole, whole],
                out_specs=whole,
                out_shape=jax.ShapeDtypeStruct((all_tiles, col_tiles, rank_cap, rows), bf16),
                compiler_params=params,
                name="coef",
            )(moved, right)
        with jax.named_scope(f"tiles{number}"):
            coef = coef.reshape(groups, row_tiles * col_tiles * rank_cap, rows)
            coef = lax.all_to_all(
                coef, ("tcol", "trow"), split_axis=0, concat_axis=0, tiled=True
            ).reshape(groups, row_tiles, col_tiles * rank_cap, rows)
        with jax.named_scope(f"reply{number}"):
            replies = pl.pallas_call(
                functools.partial(reply_kernel, sign, points),
                in_specs=[whole, whole],
                out_specs=whole,
                out_shape=rows_shape,
                compiler_params=params,
                name="reply",
            )(coef, left)
        with jax.named_scope(f"to_point{number}"):
            replies = lax.all_to_all(
                replies.reshape(freqs, 2 * points, src_rows), "freq",
                split_axis=0, concat_axis=0, tiled=True,
            ).reshape(rows, src_rows)
        if number == 0:
            with jax.named_scope("middle"):
                done, spectrum = pl.pallas_call(
                    functools.partial(middle_kernel, back_scale, scale),
                    grid=(chunks,),
                    in_specs=[table_spec, rows_spec, window_spec],
                    out_specs=(field_spec, rows_spec),
                    out_shape=(pass_shape, rows_shape),
                    compiler_params=params,
                    name="middle",
                )(table, replies, window)
        else:
            with jax.named_scope("last"):
                done = pl.pallas_call(
                    functools.partial(last_kernel, back_scale),
                    grid=(chunks,),
                    in_specs=[table_spec, rows_spec, window_spec],
                    out_specs=field_spec,
                    out_shape=pass_shape,
                    compiler_params=params,
                    name="last",
                )(table, replies, window)
        outputs.append(done)
    return (outputs[0], outputs[1])


def solution(mesh):
    in_specs = (
        P("freq", ("tcol", "trow"), None),
        P("freq", ("tcol", "trow")),
        P("freq", None, ("tcol", "trow")),
        P("freq", ("tcol", "trow"), None, None, None, None),
        P("freq", None, ("tcol", "trow"), None, None, None),
    )
    out_specs = (P("freq", ("tcol", "trow"), None), P("freq", ("tcol", "trow"), None))
    return jax.shard_map(body, mesh=mesh, in_specs=in_specs, out_specs=out_specs, check_vma=False)
```

time: 176 us -> 156 us (0.89)
  blocking collectives: 107 us -> 81.2 us
  Pallas kernels: 0 us -> 24 us
  matrix products: 20.5 us -> 0 us
  other arithmetic: 11.1 us -> 0.01 us
  waiting for transfers between devices: 14.7 us -> 19.7 us
  starting transfers between devices: 11.4 us -> 15.7 us
  local copies, waits for them, and re-layouts: 10.5 us -> 13.9 us
    all_to_all x5 -> x4, blocking collectives: 107 us -> 81.2 us  [the longest x2 38.4 us: body(): lax.all_to_all(replies.reshape(freqs, 2 * points, src_rows), 'freq', spli...]
    pallas_call x0 -> x9, Pallas kernels: none -> 24 us  [the longest x1 5.28 us: body(): pl.pallas_call(right_kernel, in_specs=[smem, whole], out_specs=whole, out...]
    dot_general x8 -> x0, matrix products: 20.5 us -> none  [the longest x2 7.62 us: body(): jnp.einsum('fijkcl,fijkdp->cdfpil', left_factors, gathered, preferred_ele...]
    unnamed x6 -> x26, local copies, waits for them, and re-layouts: 0.02 us -> 13.8 us
    convert_element_type x2 -> x0, other arithmetic: 9.32 us -> none  [body(): coefficients.astype(jnp.bfloat16)]
    another operation x12 -> x0, local copies, waits for them, and re-layouts: 7.72 us -> none  [the longest x2 4.97 us: body(): stacked = jnp.stack([real_part, imag_part], axis=4)]
    all_to_all x1 -> x2, waiting for transfers between devices: 14.7 us -> 19.7 us  [the longest x1 14.7 us: body(): lax.all_to_all(coef, ('tcol', 'trow'), split_axis=0, concat_axis=0, tiled...]
    all_to_all x1 -> x2, starting transfers between devices: 11.4 us -> 15.7 us  [the longest x1 11.4 us: body(): lax.all_to_all(spectrum.reshape(freqs, 2 * points, src_rows), 'freq', spl...]
  transfers between devices with their start and end apart: 1 -> 2, of which waited for: 1 -> 2; matrix products, arithmetic and copies ran while one was open for 0% -> 0% of each run, Pallas kernels for 0% -> 5%
where the time goes in v1:
time: 156 us; the launch traced here: 155 us
  blocking collectives  81.2 us (52%)
  Pallas kernels  24 us (15%)
  waiting for transfers between devices  19.7 us (13%)
  starting transfers between devices  15.7 us (10%)
  local copies, waits for them, and re-layouts  13.9 us (9%)
    all_to_all x2, blocking collectives, body(): lax.all_to_all(replies.reshape(freqs, 2 * points, src_rows), 'freq', spli...  38.4 us
    all_to_all x1, blocking collectives, body(): lax.all_to_all(coef, ('tcol', 'trow'), split_axis=0, concat_axis=0, tiled...  24 us
    all_to_all x1, blocking collectives, body(): lax.all_to_all(spectrum.reshape(freqs, 2 * points, src_rows), 'freq', spl...  18.8 us
    all_to_all x1, waiting for transfers between devices, body(): lax.all_to_all(coef, ('tcol', 'trow'), split_axis=0, concat_axis=0, tiled...  14.7 us
    unnamed x26, local copies, waits for them, and re-layouts  13.8 us
    all_to_all x1, starting transfers between devices, body(): lax.all_to_all(spectrum.reshape(freqs, 2 * points, src_rows), 'freq', spl...  11.4 us
    pallas_call x1, Pallas kernels, body(): pl.pallas_call(right_kernel, in_specs=[smem, whole], out_specs=whole, out...  5.28 us
    all_to_all x1, waiting for transfers between devices, body(): lax.all_to_all(spectrum.reshape(freqs, 2 * points, src_rows), 'freq', spl...  5.02 us
  transfers between devices with their start and end apart: 2, of which 2 were waited for; matrix products, arithmetic and copies ran while one was open for 0% of the time, Pallas kernels for 5%

profile of v1, /device:TPU:32, one launch (start us, length us, event | category | flops | bytes accessed | tf_op | source)
XLA Modules:
  0.0 155.3 jit_solution(7723715138982631718)
XLA Ops:
  0.6 4.0 %dft_first.1 = bf16[256,768]{1,0:T(8,128)(2,1)} custom-call(bf16[256,256]{1,0:T(8,128)(2,1)} %constant.8.table_ref, bf16[4,768,256]{2,1,0:T(8,128)(2,1)} %field_ref.1, s32[4,768]{1,0:T(4,128)} %window_ref.5), custom_call_target="tpu_custom_call" | custom-call | tf_op jit(solution)/shard_map/dft_first/dft_first/pallas_call | solution.py:217
  4.6 11.4 %all-to-all-start = ((bf16[32,8,768]{2,1,0:T(8,128)(2,1)}), bf16[32,8,768]{2,1,0:T(8,128)(2,1)S(1)}, u32[]{:S(2)}, u32[]{:S(2)}) async-start(bf16[32,8,768]{2,1,0:T(8,128)(2,1)} %bitcast.27), calls=%async_computation | async-start | bytes 786432 | tf_op jit(solution)/shard_map/to_freq0/all_to_all | solution.py:230
  16.0 0.1 copy.8.rank_ref
  16.1 2.3 %copy-done.5 = bf16[1,16,2,96,2,384]{5,4,3,2,1,0:T(2,128)(2,1)S(1)} copy-done((bf16[1,16,2,96,2,384]{5,4,3,2,1,0:T(2,128)(2,1)S(1)}, bf16[1,16,2,96,2,384]{5,4,3,2,1,0:T(2,128)(2,1)}, u32[]{:S(2)}) %copy-start.5) | copy-done | bytes 4718616
  18.4 5.3 %prep_right.1.right_ref = bf16[2,1536,768]{2,1,0:T(8,128)(2,1)S(1)} custom-call(s32[16,2]{1,0:T(8,128)S(1)} %copy.8.rank_ref, bf16[1,16,2,96,2,384]{5,4,3,2,1,0:T(2,128)(2,1)S(1)} %copy-done.5), custom_call_target="tpu_custom_call" | custom-call | tf_op jit(solution)/shard_map/prep_right/prep_right/pallas_call | solution.py:194
  23.7 2.1 %copy-done = bf16[2,1536,768]{2,1,0:T(8,128)(2,1)} copy-done((bf16[2,1536,768]{2,1,0:T(8,128)(2,1)}, bf16[2,1536,768]{2,1,0:T(8,128)(2,1)S(1)}, u32[]{:S(2)}) %copy-start) | copy-done | bytes 4718616
  25.9 5.0 %all-to-all-done = bf16[32,8,768]{2,1,0:T(8,128)(2,1)S(1)} async-done(((bf16[32,8,768]{2,1,0:T(8,128)(2,1)}), bf16[32,8,768]{2,1,0:T(8,128)(2,1)S(1)}, u32[]{:S(2)}, u32[]{:S(2)}) %all-to-all-start) | async-done | bytes 393248 | tf_op jit(solution)/shard_map/to_freq0/all_to_all | solution.py:230
  30.9 2.3 %copy-done.1 = bf16[2,1536,768]{2,1,0:T(8,128)(2,1)S(1)} copy-done((bf16[2,1536,768]{2,1,0:T(8,128)(2,1)S(1)}, bf16[2,1536,768]{2,1,0:T(8,128)(2,1)}, u32[]{:S(2)}) %copy-start.1) | copy-done | bytes 4718616
  33.2 2.6 %coef.2 = bf16[16,2,96,256]{3,2,1,0:T(8,128)(2,1)} custom-call(bf16[256,768]{1,0:T(8,128)(2,1)S(1)} %bitcast.20, bf16[2,1536,768]{2,1,0:T(8,128)(2,1)S(1)} %copy-done.1), custom_call_target="tpu_custom_call" | custom-call | tf_op jit(solution)/shard_map/coef0/coef/pallas_call | solution.py:235
  35.8 4.3 %all-to-all-start.1 = ((bf16[8,384,256]{2,1,0:T(8,128)(2,1)}), bf16[8,384,256]{2,1,0:T(8,128)(2,1)S(1)}, u32[]{:S(2)}, u32[]{:S(2)}) async-start(bf16[8,384,256]{2,1,0:T(8,128)(2,1)} %bitcast.3), calls=%async_computation.1 | async-start | bytes 3145728 | tf_op jit(solution)/shard_map/tiles0/all_to_all | solution.py:245
  40.1 2.3 %copy-done.4 = bf16[1,2,16,96,2,384]{5,4,3,2,1,0:T(2,128)(2,1)S(1)} copy-done((bf16[1,2,16,96,2,384]{5,4,3,2,1,0:T(2,128)(2,1)S(1)}, bf16[1,2,16,96,2,384]{5,4,3,2,1,0:T(2,128)(2,1)}, u32[]{:S(2)}) %copy-start.4) | copy-done | bytes 4718616
  42.4 2.3 %prep_left.1.left_ref = bf16[2,1536,768]{2,1,0:T(8,128)(2,1)S(1)} custom-call(bf16[1,2,16,96,2,384]{5,4,3,2,1,0:T(2,128)(2,1)S(1)} %copy-done.4), custom_call_target="tpu_custom_call" | custom-call | tf_op jit(solution)/shard_map/prep_left/prep_left/pallas_call | solution.py:205
  44.7 2.2 %copy-done.2 = bf16[2,1536,768]{2,1,0:T(8,128)(2,1)} copy-done((bf16[2,1536,768]{2,1,0:T(8,128)(2,1)}, bf16[2,1536,768]{2,1,0:T(8,128)(2,1)S(1)}, u32[]{:S(2)}) %copy-start.2) | copy-done | bytes 4718616
  46.9 14.7 %all-to-all-done.1 = bf16[8,384,256]{2,1,0:T(8,128)(2,1)S(1)} async-done(((bf16[8,384,256]{2,1,0:T(8,128)(2,1)}), bf16[8,384,256]{2,1,0:T(8,128)(2,1)S(1)}, u32[]{:S(2)}, u32[]{:S(2)}) %all-to-all-start.1) | async-done | bytes 1572896 | tf_op jit(solution)/shard_map/tiles0/all_to_all | solution.py:245
  61.6 2.5 %copy-done.3 = bf16[2,1536,768]{2,1,0:T(8,128)(2,1)S(1)} copy-done((bf16[2,1536,768]{2,1,0:T(8,128)(2,1)S(1)}, bf16[2,1536,768]{2,1,0:T(8,128)(2,1)}, u32[]{:S(2)}) %copy-start.3) | copy-done | bytes 4718616
  64.1 1.4 reply.2
  65.6 19.3 %all_to_all.30 = bf16[32,8,768]{2,1,0:T(8,128)(2,1)S(1)} all-to-all(bf16[32,8,768]{2,1,0:T(8,128)(2,1)S(1)} %bitcast.25), channel_id=1, replica_groups=mesh['freq'=32,'tcol'=4,'trow'=2] {'freq'}, dimensions={0} | all-to-all | bytes 786432 | tf_op jit(solution)/shard_map/to_point0/all_to_all | solution.py:258
  84.9 3.1 %middle.1 = (bf16[4,768,256]{2,1,0:T(8,128)(2,1)}, bf16[256,768]{1,0:T(8,128)(2,1)S(1)}) custom-call(bf16[256,256]{1,0:T(8,128)(2,1)S(1)} %copy-done.6, bf16[256,768]{1,0:T(8,128)(2,1)S(1)} %bitcast.21, s32[4,768]{1,0:T(4,128)S(1)} %copy-done.7), custom_call_target="tpu_custom_call" | custom-call | tf_op jit(solution)/shard_map/middle/middle/pallas_call | solution.py:264
  88.0 18.8 %all_to_all.31 = bf16[32,8,768]{2,1,0:T(8,128)(2,1)S(1)} all-to-all(bf16[32,8,768]{2,1,0:T(8,128)(2,1)S(1)} %bitcast.26), channel_id=1, replica_groups=mesh['freq'=32,'tcol'=4,'trow'=2] {'freq'}, dimensions={0} | all-to-all | bytes 786432 | tf_op jit(solution)/shard_map/to_freq1/all_to_all | solution.py:230
  106.8 1.5 coef.3
  108.2 24.0 %all_to_all.32 = bf16[8,384,256]{2,1,0:T(8,128)(2,1)S(1)} all-to-all(bf16[8,384,256]{2,1,0:T(8,128)(2,1)S(1)} %bitcast.18), channel_id=1, replica_groups=mesh['freq'=32,'tcol'=4,'trow'=2] {'tcol','trow'}, dimensions={0} | all-to-all | bytes 3145728 | tf_op jit(solution)/shard_map/tiles1/all_to_all | solution.py:245
  132.3 1.4 reply.3
  133.7 19.1 %all_to_all.33 = bf16[32,8,768]{2,1,0:T(8,128)(2,1)S(1)} all-to-all(bf16[32,8,768]{2,1,0:T(8,128)(2,1)S(1)} %bitcast.23), channel_id=1, replica_groups=mesh['freq'=32,'tcol'=4,'trow'=2] {'freq'}, dimensions={0} | all-to-all | bytes 786432 | tf_op jit(solution)/shard_map/to_point1/all_to_all | solution.py:258
  152.8 2.4 %last.1 = bf16[4,768,256]{2,1,0:T(8,128)(2,1)} custom-call(bf16[256,256]{1,0:T(8,128)(2,1)S(1)} %copy-done.6, bf16[256,768]{1,0:T(8,128)(2,1)S(1)} %bitcast.24, s32[4,768]{1,0:T(4,128)S(1)} %copy-done.7), custom_call_target="tpu_custom_call" | custom-call | tf_op jit(solution)/shard_map/last/last/pallas_call | solution.py:275
  (22 shorter events, 0.0 us)
Async XLA Ops:
  0.6 15.4 %copy-start.8 = (s32[1,16,2]{1,2,0:T(2,128)S(1)}, s32[1,16,2]{1,2,0:T(2,128)}, u32[]{:S(2)}) copy-start(s32[1,16,2]{1,2,0:T(2,128)} %param.8) | copy-start | bytes 388
  4.6 26.2 %all-to-all-start = ((bf16[32,8,768]{2,1,0:T(8,128)(2,1)}), bf16[32,8,768]{2,1,0:T(8,128)(2,1)S(1)}, u32[]{:S(2)}, u32[]{:S(2)}) async-start(bf16[32,8,768]{2,1,0:T(8,128)(2,1)} %bitcast.27), calls=%async_computation | async-start | bytes 786432 | tf_op jit(solution)/shard_map/to_freq0/all_to_all | solution.py:230
  16.1 2.3 %copy-start.5 = (bf16[1,16,2,96,2,384]{5,4,3,2,1,0:T(2,128)(2,1)S(1)}, bf16[1,16,2,96,2,384]{5,4,3,2,1,0:T(2,128)(2,1)}, u32[]{:S(2)}) copy-start(bf16[1,16,2,96,2,384]{5,4,3,2,1,0:T(2,128)(2,1)} %factor_ref.2) | copy-start | bytes 14155780
  23.7 2.1 %copy-start = (bf16[2,1536,768]{2,1,0:T(8,128)(2,1)}, bf16[2,1536,768]{2,1,0:T(8,128)(2,1)S(1)}, u32[]{:S(2)}) copy-start(bf16[2,1536,768]{2,1,0:T(8,128)(2,1)S(1)} %prep_right.1.right_ref) | copy-start | bytes 14155780
  30.9 2.3 %copy-start.1 = (bf16[2,1536,768]{2,1,0:T(8,128)(2,1)S(1)}, bf16[2,1536,768]{2,1,0:T(8,128)(2,1)}, u32[]{:S(2)}) copy-start(bf16[2,1536,768]{2,1,0:T(8,128)(2,1)} %copy-done) | copy-start | bytes 14155780
  35.8 25.8 %all-to-all-start.1 = ((bf16[8,384,256]{2,1,0:T(8,128)(2,1)}), bf16[8,384,256]{2,1,0:T(8,128)(2,1)S(1)}, u32[]{:S(2)}, u32[]{:S(2)}) async-start(bf16[8,384,256]{2,1,0:T(8,128)(2,1)} %bitcast.3), calls=%async_computation.1 | async-start | bytes 3145728 | tf_op jit(solution)/shard_map/tiles0/all_to_all | solution.py:245
  40.1 2.3 %copy-start.4 = (bf16[1,2,16,96,2,384]{5,4,3,2,1,0:T(2,128)(2,1)S(1)}, bf16[1,2,16,96,2,384]{5,4,3,2,1,0:T(2,128)(2,1)}, u32[]{:S(2)}) copy-start(bf16[1,2,16,96,2,384]{5,4,3,2,1,0:T(2,128)(2,1)} %factor_ref.3) | copy-start | bytes 14155780
  44.7 2.2 %copy-start.2 = (bf16[2,1536,768]{2,1,0:T(8,128)(2,1)}, bf16[2,1536,768]{2,1,0:T(8,128)(2,1)S(1)}, u32[]{:S(2)}) copy-start(bf16[2,1536,768]{2,1,0:T(8,128)(2,1)S(1)} %prep_left.1.left_ref) | copy-start | bytes 14155780
  61.6 45.1 %slice-start = ((s8[4718592]{0:T(1024)(128)(4,1)}), s8[4194304]{0:T(1024)(128)(4,1)S(1)}, s32[]{:S(2)}) async-start(s8[4718592]{0:T(1024)(128)(4,1)} %bitcast.13), calls=%async_computation.6 | async-start | bytes 8388608
  61.6 2.5 %copy-start.3 = (bf16[2,1536,768]{2,1,0:T(8,128)(2,1)S(1)}, bf16[2,1536,768]{2,1,0:T(8,128)(2,1)}, u32[]{:S(2)}) copy-start(bf16[2,1536,768]{2,1,0:T(8,128)(2,1)} %copy-done.2) | copy-start | bytes 14155780
  64.1 20.7 %copy-start.6 = (bf16[256,256]{1,0:T(8,128)(2,1)S(1)}, bf16[256,256]{1,0:T(8,128)(2,1)}, u32[]{:S(2)}) copy-start(bf16[256,256]{1,0:T(8,128)(2,1)} %constant.8.table_ref) | copy-start | bytes 393220
  64.1 20.7 %copy-start.7 = (s32[4,768]{1,0:T(4,128)S(1)}, s32[4,768]{1,0:T(4,128)}, u32[]{:S(2)}) copy-start(s32[4,768]{1,0:T(4,128)} %window_ref.5) | copy-start | bytes 36868
  64.1 42.6 %slice-start.1 = ((s8[4718592]{0:T(1024)(128)(4,1)}), s8[524288]{0:T(1024)(128)(4,1)S(1)}, s32[]{:S(2)}) async-start(s8[4718592]{0:T(1024)(128)(4,1)} %bitcast.13), calls=%async_computation.7 | async-start | bytes 1048576
  87.9 44.3 %slice-start.2 = ((s8[4718592]{0:T(1024)(128)(4,1)}), s8[4194304]{0:T(1024)(128)(4,1)S(1)}, s32[]{:S(2)}) async-start(s8[4718592]{0:T(1024)(128)(4,1)} %bitcast.15), calls=%async_computation.8 | async-start | bytes 8388608
  106.8 25.5 %slice-start.3 = ((s8[4718592]{0:T(1024)(128)(4,1)}), s8[524288]{0:T(1024)(128)(4,1)S(1)}, s32[]{:S(2)}) async-start(s8[4718592]{0:T(1024)(128)(4,1)} %bitcast.15), calls=%async_computation.9 | async-start | bytes 1048576

commit v2 on v0

v2 whole, which is shorter than its diff:
```python
import functools
import math

import jax
import jax.numpy as jnp
import numpy as np
from jax import lax
from jax.experimental import pallas as pl
from jax.experimental.pallas import tpu as pltpu
from jax.sharding import PartitionSpec as P


MIB = 1 << 20
PARTNERS = ((2, 0), (1, 0), (3, 0), (2, 1), (1, 1), (3, 1), (0, 1), (0, 0))
SPLIT = 5
CALLS = ((0, 2), (2, 5), (5, 8))
EARLY = (7, 6, 0, 1)
LATE = (2, 3, 4, 5)


def spectral_rows(count_freq, time_len, repeat):
    row = np.arange(count_freq * 2 * repeat)
    bins = row // (2 * repeat) + 1
    part = (row // repeat) % 2
    turns = bins[:, None] * np.arange(time_len)[None, :] % time_len
    phase = turns.astype(np.float32) * np.float32(2.0 * math.pi / time_len)
    table = np.where(part[:, None] == 0, np.cos(phase), -np.sin(phase))
    return jnp.asarray(table.astype(np.float32)).astype(jnp.bfloat16)


def nt_dot(a, b):
    return lax.dot_general(a, b, (((1,), (1,)), ((), ())), preferred_element_type=jnp.float32)


def tn_dot(a, b):
    return lax.dot_general(a, b, (((0,), (0,)), ((), ())), preferred_element_type=jnp.float32)


def swap_parts(x, half):
    rows, cols = x.shape
    grouped = x.reshape(rows // (2 * half), 2 * half, cols)
    return pltpu.roll(grouped, half, axis=1).reshape(rows, cols)


def part_sign(shape, half, sign):
    row = lax.broadcasted_iota(jnp.int32, shape, 0)
    return jnp.where(row % (2 * half) < half, sign, -sign).astype(jnp.float32)


def spread_table(table, points, scale):
    row = lax.broadcasted_iota(jnp.int32, table.shape, 0) % points
    scaled = table * jnp.asarray(scale, table.dtype)
    return jnp.concatenate(
        [jnp.where(row == point, scaled, jnp.zeros_like(table)) for point in range(points)], axis=1
    )


def stand_window(window):
    wide = window.astype(jnp.float32)
    padded = jnp.concatenate([wide, jnp.zeros((8 - wide.shape[0], wide.shape[1]), jnp.float32)])
    return padded.T


def mute(block, window):
    rows, length = block.shape
    lanes = 128
    limit = jnp.broadcast_to(window, (rows, lanes)).astype(jnp.bfloat16)
    kept = []
    for start in range(0, length, lanes):
        at = lax.broadcasted_iota(jnp.int32, (rows, lanes), 1) + start
        part = block[:, start : start + lanes]
        kept.append(jnp.where(at.astype(jnp.bfloat16) < limit, part, jnp.zeros_like(part)))
    return jnp.concatenate(kept, axis=1)


def to_freq(table, signals):
    return nt_dot(table, jnp.concatenate(signals, axis=1)).astype(jnp.bfloat16)


def to_time(table, replies, window, points):
    waves = tn_dot(replies, table).astype(jnp.bfloat16)
    length = waves.shape[1] // points
    return [
        mute(waves[:, p * length : (p + 1) * length], window[:, p : p + 1])
        for p in range(points)
    ]


def first_kernel(
    scale, step, table_hbm, window_hbm, field_hbm, out_ref, table_ref, window_ref, field_ref, sems
):
    points, src_rows, _ = field_ref.shape
    small = [
        pltpu.make_async_copy(window_hbm, window_ref, sems.at[points]),
        pltpu.make_async_copy(table_hbm, table_ref, sems.at[points + 1]),
    ]
    copies = [
        pltpu.make_async_copy(field_hbm.at[point], field_ref.at[point], sems.at[point])
        for point in range(points)
    ]
    for copy in small + copies:
        copy.start()
    small[0].wait()
    window = stand_window(window_ref[...])
    small[1].wait()
    table = spread_table(table_ref[...], points, scale)
    for copy in copies:
        copy.wait()
    for start in range(0, src_rows, step):
        signals = [
            mute(
                field_ref[point, start : start + step],
                window[start : start + step, point : point + 1],
            )
            for point in range(points)
        ]
        out_ref[:, start : start + step] = to_freq(table, signals)


def middle_kernel(back_scale, scale, step, table_ref, window_ref, reply_ref, pass_ref, out_ref):
    points, src_rows, _ = pass_ref.shape
    back = spread_table(table_ref[...], points, back_scale)
    table = spread_table(table_ref[...], points, scale)
    window = stand_window(window_ref[...])
    for start in range(0, src_rows, step):
        blocks = to_time(
            back, reply_ref[:, start : start + step], window[start : start + step], points
        )
        for point in range(points):
            pass_ref[point, start : start + step] = blocks[point]
        out_ref[:, start : start + step] = to_freq(table, blocks)


def last_kernel(back_scale, step, table_ref, window_ref, reply_ref, pass_hbm, pass_ref, sems):
    points, src_rows, _ = pass_ref.shape
    table = spread_table(table_ref[...], points, back_scale)
    window = stand_window(window_ref[...])
    copies = []
    for number, start in enumerate(range(0, src_rows, step)):
        part = pl.ds(start, step)
        blocks = to_time(
            table, reply_ref[:, start : start + step], window[start : start + step], points
        )
        for point in range(points):
            pass_ref[point, start : start + step] = blocks[point]
            copies.append(
                pltpu.make_async_copy(
                    pass_ref.at[point, part, :], pass_hbm.at[point, part, :],
                    sems.at[number, point],
                )
            )
            copies[-1].start()
    for copy in copies:
        copy.wait()


def right_kernel(place_ref, rank_ref, factor_ref, early_ref, late_ref):
    _, all_tiles, col_tiles, rank_cap, parts, tile_len = factor_ref.shape
    row_tiles = all_tiles // len(PARTNERS)
    block = 16

    def fill(out_ref, first):
        def one_tile(number, carry):
            at, col = number // col_tiles, number % col_tiles
            slot = at // row_tiles + first
            tile = place_ref[slot] * row_tiles + at % row_tiles
            rank = rank_ref[tile, col]
            for start in range(0, rank_cap, block):
                rows = pl.ds(pl.multiple_of(at * rank_cap + start, block), block)

                @pl.when(start < rank)
                def _():
                    part = factor_ref[0, tile, col, start : start + block]
                    part = part.reshape(block, parts * tile_len)
                    row = lax.broadcasted_iota(jnp.int32, part.shape, 0) + start
                    out_ref[col, rows] = jnp.where(row < rank, part, jnp.zeros_like(part))

                @pl.when(start >= rank)
                def _():
                    out_ref[col, rows] = jnp.zeros((block, parts * tile_len), out_ref.dtype)

            return carry

        lax.fori_loop(0, out_ref.shape[1] // rank_cap * col_tiles, one_tile, 0)

    fill(early_ref, 0)
    fill(late_ref, SPLIT)


def left_kernel(place_ref, factor_ref, out_ref):
    _, row_tiles, all_tiles, rank_cap, parts, tile_len = factor_ref.shape
    col_tiles = all_tiles // len(PARTNERS)

    def one_tile(number, carry):
        tile, at = number // all_tiles, number % all_tiles
        col = place_ref[at // col_tiles] * col_tiles + at % col_tiles
        part = factor_ref[0, tile, col].reshape(rank_cap, parts * tile_len)
        out_ref[tile, pl.ds(pl.multiple_of(at * rank_cap, 16), rank_cap)] = part
        return carry

    lax.fori_loop(0, row_tiles * all_tiles, one_tile, 0)


def coef_kernel(sign, half, first, spec_ref, right_ref, *outs):
    row_tiles, depth, _ = outs[0].shape
    col_tiles = right_ref.shape[0]
    rank_cap = depth // col_tiles
    tile_len = spec_ref.shape[1] // col_tiles
    for col in range(col_tiles):
        block = spec_ref[:, col * tile_len : (col + 1) * tile_len]
        wide = block.astype(jnp.float32)
        other = swap_parts(wide, half) * part_sign(wide.shape, half, sign)
        paired = jnp.concatenate([block, other.astype(jnp.bfloat16)], axis=1)
        span = row_tiles * rank_cap
        factors = right_ref[col, first * span : (first + len(outs)) * span]
        coef = nt_dot(factors, paired).astype(jnp.bfloat16)
        for number in range(len(outs)):
            for tile in range(row_tiles):
                start = (number * row_tiles + tile) * rank_cap
                outs[number][tile, col * rank_cap : (col + 1) * rank_cap] = coef[
                    start : start + rank_cap
                ]


def reply_sum(first, coef_refs, left_ref, tile):
    depth = coef_refs[0].shape[1]
    coef = jnp.concatenate([ref[tile] for ref in coef_refs], axis=0)
    return tn_dot(coef, left_ref[tile, first * depth : (first + len(coef_refs)) * depth])


def early_kernel(*refs):
    *coef_refs, left_ref, out_ref = refs
    for tile in range(out_ref.shape[0]):
        out_ref[tile] = reply_sum(0, coef_refs, left_ref, tile)


def late_kernel(sign, half, *refs):
    *coef_refs, left_ref, sum_ref, out_ref = refs
    tile_len = sum_ref.shape[2] // 2
    for tile in range(sum_ref.shape[0]):
        both = reply_sum(len(EARLY), coef_refs, left_ref, tile) + sum_ref[tile]
        other = both[:, tile_len:]
        other = swap_parts(other, half) * part_sign(other.shape, half, -sign)
        reply = both[:, :tile_len] + other
        out_ref[:, tile * tile_len : (tile + 1) * tile_len] = reply.astype(jnp.bfloat16)


def body(focal_field, mute_window, tile_ranks, left_factors, right_factors):
    points, src_rows, time_len = focal_field.shape
    _, row_tiles, all_tiles, rank_cap, parts_two, tile_len = left_factors.shape
    col_tiles = right_factors.shape[2]
    freqs = lax.axis_size("freq")
    chips, cores = lax.axis_size("tcol"), lax.axis_size("trow")
    rows = freqs * 2 * points
    depth = col_tiles * rank_cap
    table = spectral_rows(freqs, time_len, points)
    scale = 1.0 / math.sqrt(time_len)
    back_scale = 2.0 / math.sqrt(time_len)
    step = 256
    chunks = src_rows // step
    bf16 = jnp.bfloat16
    dma = pltpu.SemaphoreType.DMA

    whole = pl.BlockSpec(memory_space=pltpu.VMEM)
    smem = pl.BlockSpec(memory_space=pltpu.SMEM)
    anywhere = pl.BlockSpec(memory_space=pl.ANY)
    params = pltpu.CompilerParams(vmem_limit_bytes=24 * MIB)
    rows_shape = jax.ShapeDtypeStruct((rows, src_rows), bf16)
    pass_shape = jax.ShapeDtypeStruct(focal_field.shape, bf16)

    def cost(flops, moved):
        return pl.CostEstimate(flops=flops, bytes_accessed=moved, transcendentals=0)

    steps = np.array([s for s, _ in PARTNERS], np.int32)
    other_core = np.array([c for _, c in PARTNERS], np.int32)
    chip, core = lax.axis_index("tcol"), lax.axis_index("trow")
    core_at = jnp.bitwise_xor(core, other_core)
    targets = (chip + steps) % chips * cores + core_at
    order = np.array(EARLY + LATE)
    arriving = jnp.bitwise_xor(core, other_core[order])
    sources = (chip + chips - steps[order]) % chips * cores + arriving
    pairs = []
    for hop, cross in PARTNERS[:-1]:
        pairs.append(
            [
                (x * cores + c, (x + hop) % chips * cores + (c ^ cross))
                for x in range(chips)
                for c in range(cores)
            ]
        )

    factor_size = all_tiles * col_tiles * rank_cap * parts_two * tile_len
    shapes = [
        (col_tiles, count * row_tiles * rank_cap, parts_two * tile_len)
        for count in (SPLIT, len(PARTNERS) - SPLIT)
    ]
    right = pl.pallas_call(
        right_kernel,
        in_specs=[smem, smem, whole],
        out_specs=[whole, whole],
        out_shape=[jax.ShapeDtypeStruct(shape, bf16) for shape in shapes],
        compiler_params=params,
        cost_estimate=cost(0, 6 * factor_size),
        name="prep_right",
    )(targets, tile_ranks.reshape(all_tiles, col_tiles), right_factors)
    spectrum = pl.pallas_call(
        functools.partial(first_kernel, scale, step),
        in_specs=[anywhere, anywhere, anywhere],
        out_specs=whole,
        out_shape=rows_shape,
        scratch_shapes=[
            pltpu.VMEM(table.shape, bf16),
            pltpu.VMEM(mute_window.shape, jnp.int32),
            pltpu.VMEM(focal_field.shape, bf16),
            dma((points + 2,)),
        ],
        compiler_params=pltpu.CompilerParams(vmem_limit_bytes=58 * MIB),
        name="dft_first",
    )(table, mute_window, focal_field)

    def coefficients(sign, moved, begin, end):
        count = end - begin
        factors, first = (right[0], begin) if end <= SPLIT else (right[1], begin - SPLIT)
        return pl.pallas_call(
            functools.partial(coef_kernel, sign, points, first),
            in_specs=[whole, whole],
            out_specs=[whole] * count,
            out_shape=[jax.ShapeDtypeStruct((row_tiles, depth, rows), bf16)] * count,
            compiler_params=params,
            cost_estimate=cost(
                2 * count * row_tiles * depth * parts_two * tile_len * rows,
                count * factor_size // 4,
            ),
            name="coef",
        )(moved, factors)

    def reply_call(kernel, count, out_shape, operands):
        return pl.pallas_call(
            kernel,
            in_specs=[whole] * len(operands),
            out_specs=whole,
            out_shape=out_shape,
            compiler_params=params,
            cost_estimate=cost(
                2 * count * row_tiles * depth * parts_two * tile_len * rows,
                count * factor_size // 4,
            ),
            name="reply",
        )(*operands)

    outputs = []
    outputs = []
    for number, sign in enumerate((1.0, -1.0)):
        moved = lax.all_to_all(
            spectrum.reshape(freqs, 2 * points, src_rows), "freq",
            split_axis=0, concat_axis=0, tiled=True,
        ).reshape(rows, src_rows)
        if number == 0:
            left = pl.pallas_call(
                left_kernel,
                in_specs=[smem, whole],
                out_specs=whole,
                out_shape=jax.ShapeDtypeStruct(
                    (row_tiles, all_tiles * rank_cap, parts_two * tile_len), bf16
                ),
                compiler_params=params,
                cost_estimate=cost(0, 6 * factor_size),
                name="prep_left",
            )(sources, left_factors)
        blocks = []
        for begin, end in CALLS:
            blocks += coefficients(sign, moved, begin, end)
        arrived = []
        for slot, pair in enumerate(pairs):
            arrived.append(lax.ppermute(blocks[slot], ("tcol", "trow"), pair))
        arrived.append(blocks[-1])
        part = reply_call(
            early_kernel, len(EARLY),
            jax.ShapeDtypeStruct((row_tiles, rows, parts_two * tile_len), jnp.float32),
            [arrived[slot] for slot in EARLY] + [left],
        )
        replies = reply_call(
            functools.partial(late_kernel, sign, points), len(LATE), rows_shape,
            [arrived[slot] for slot in LATE] + [left, part],
        )
        replies = lax.all_to_all(
            replies.reshape(freqs, 2 * points, src_rows), "freq",
            split_axis=0, concat_axis=0, tiled=True,
        ).reshape(rows, src_rows)
        if number == 0:
            done, spectrum = pl.pallas_call(
                functools.partial(middle_kernel, back_scale, scale, step),
                in_specs=[whole, whole, whole],
                out_specs=(whole, whole),
                out_shape=(pass_shape, rows_shape),
                compiler_params=params,
                name="middle",
            )(table, mute_window, replies)
        else:
            done = pl.pallas_call(
                functools.partial(last_kernel, back_scale, step),
                in_specs=[whole, whole, whole],
                out_specs=anywhere,
                out_shape=pass_shape,
                scratch_shapes=[pltpu.VMEM(pass_shape.shape, bf16), dma((chunks, points))],
                compiler_params=params,
                name="last",
            )(table, mute_window, replies)
        outputs.append(done)
    return (outputs[0], outputs[1])


def solution(mesh):
    in_specs = (
        P("freq", ("tcol", "trow"), None),
        P("freq", ("tcol", "trow")),
        P("freq", None, ("tcol", "trow")),
        P("freq", ("tcol", "trow"), None, None, None, None),
        P("freq", None, ("tcol", "trow"), None, None, None),
    )
    out_specs = (P("freq", ("tcol", "trow"), None), P("freq", ("tcol", "trow"), None))
    return jax.shard_map(body, mesh=mesh, in_specs=in_specs, out_specs=out_specs, check_vma=False)
```

time: 176 us -> 140 us (0.80)
  blocking collectives: 107 us -> 58.5 us
  Pallas kernels: 0 us -> 24.1 us
  matrix products: 20.5 us -> 0 us
  starting transfers between devices: 11.4 us -> 29.6 us
  other arithmetic: 11.1 us -> 0.02 us
  waiting for transfers between devices: 14.7 us -> 21.5 us
  local copies, waits for them, and re-layouts: 10.5 us -> 5.17 us
    all_to_all x5 -> x3, blocking collectives: 107 us -> 58.5 us  [the longest x2 39.5 us: body(): lax.all_to_all(replies.reshape(freqs, 2 * points, src_rows), 'freq', spli...]
    pallas_call x0 -> x15, Pallas kernels: none -> 24.1 us  [the longest x1 5.58 us: body(): pl.pallas_call(right_kernel, in_specs=[smem, smem, whole], out_specs=[who...]
    dot_general x8 -> x0, matrix products: 20.5 us -> none  [the longest x2 7.62 us: body(): jnp.einsum('fijkcl,fijkdp->cdfpil', left_factors, gathered, preferred_ele...]
    ppermute x0 -> x14, starting transfers between devices: none -> 18.2 us  [body(): arrived.append(lax.ppermute(blocks[slot], ('tcol', 'trow'), pair))]
    ppermute x0 -> x14, waiting for transfers between devices: none -> 15.9 us  [body(): arrived.append(lax.ppermute(blocks[slot], ('tcol', 'trow'), pair))]
    convert_element_type x2 -> x0, other arithmetic: 9.32 us -> none  [body(): coefficients.astype(jnp.bfloat16)]
    all_to_all x1, waiting for transfers between devices: 14.7 us -> 5.59 us  [body(): lax.all_to_all(spectrum.reshape(freqs, 2 * points, src_rows), 'freq', spl...]
    another operation x12 -> x0, local copies, waits for them, and re-layouts: 7.72 us -> none  [the longest x2 4.97 us: body(): stacked = jnp.stack([real_part, imag_part], axis=4)]
  transfers between devices with their start and end apart: 1 -> 15, of which waited for: 1 -> 9; matrix products, arithmetic and copies ran while one was open for 0% -> 0% of each run, Pallas kernels for 0% -> 10%
where the time goes in v2:
time: 140 us
  blocking collectives  58.5 us (42%)
  starting transfers between devices  29.6 us (21%)
  Pallas kernels  24.1 us (17%)
  waiting for transfers between devices  21.5 us (15%)
  local copies, waits for them, and re-layouts  5.17 us (4%)
    all_to_all x2, blocking collectives, body(): lax.all_to_all(replies.reshape(freqs, 2 * points, src_rows), 'freq', spli...  39.5 us
    all_to_all x1, blocking collectives, body(): lax.all_to_all(spectrum.reshape(freqs, 2 * points, src_rows), 'freq', spl...  19 us
    ppermute x14, starting transfers between devices, body(): arrived.append(lax.ppermute(blocks[slot], ('tcol', 'trow'), pair))  18.2 us
    ppermute x14, waiting for transfers between devices, body(): arrived.append(lax.ppermute(blocks[slot], ('tcol', 'trow'), pair))  15.9 us
    all_to_all x1, starting transfers between devices, body(): lax.all_to_all(spectrum.reshape(freqs, 2 * points, src_rows), 'freq', spl...  11.4 us
    all_to_all x1, waiting for transfers between devices, body(): lax.all_to_all(spectrum.reshape(freqs, 2 * points, src_rows), 'freq', spl...  5.59 us
    pallas_call x1, Pallas kernels, body(): pl.pallas_call(right_kernel, in_specs=[smem, smem, whole], out_specs=[who...  5.58 us
    unnamed x24, local copies, waits for them, and re-layouts  5.09 us
  transfers between devices with their start and end apart: 15, of which 9 were waited for; matrix products, arithmetic and copies ran while one was open for 0% of the time, Pallas kernels for 10%

profile of v2, /device:TPU:32, one launch (start us, length us, event | category | flops | bytes accessed | tf_op | source)
XLA Modules:
  0.0 140.0 jit_solution(12358812353168914012)
XLA Ops:
  0.7 2.9 %dft_first.1 = bf16[256,768]{1,0:T(8,128)(2,1)} custom-call(bf16[256,256]{1,0:T(8,128)(2,1)} %constant.50.table_hbm.table_ref, s32[4,768]{1,0:T(4,128)} %window_ref.3, bf16[4,768,256]{2,1,0:T(8,128)(2,1)} %field_hbm.1), custom_call_target="tpu_custom_call" | custom-call | tf_op jit(solution)/shard_map/dft_first/pallas_call | solution.py:306
  3.6 11.4 %all-to-all-start = ((bf16[32,8,768]{2,1,0:T(8,128)(2,1)}), bf16[32,8,768]{2,1,0:T(8,128)(2,1)S(1)}, u32[]{:S(2)}, u32[]{:S(2)}) async-start(bf16[32,8,768]{2,1,0:T(8,128)(2,1)} %bitcast.20), calls=%async_computation | async-start | bytes 786432 | tf_op jit(solution)/shard_map/all_to_all | solution.py:354
  15.1 2.3 %copy-done.3 = bf16[1,16,2,96,2,384]{5,4,3,2,1,0:T(2,128)(2,1)S(1)} copy-done((bf16[1,16,2,96,2,384]{5,4,3,2,1,0:T(2,128)(2,1)S(1)}, bf16[1,16,2,96,2,384]{5,4,3,2,1,0:T(2,128)(2,1)}, u32[]{:S(2)}) %copy-start.3) | copy-done | bytes 4718616
  17.5 5.6 %prep_right.1 = (bf16[2,960,768]{2,1,0:T(8,128)(2,1)S(1)}, bf16[2,576,768]{2,1,0:T(8,128)(2,1)S(1)}) custom-call(s32[8]{0:T(128)S(1)} %fusion.2.place_ref, s32[16,2]{1,0:T(8,128)S(1)} %copy.12.rank_ref, bf16[1,16,2,96,2,384]{5,4,3,2,1,0:T(2,128)(2,1)S(1)} %copy-done.3), custom_call_target="tpu_custom_call" | custom-call | bytes 14155776 | tf_op jit(solution)/shard_map/prep_right/pallas_call | solution.py:297
  24.3 5.6 %all-to-all-done = bf16[32,8,768]{2,1,0:T(8,128)(2,1)S(1)} async-done(((bf16[32,8,768]{2,1,0:T(8,128)(2,1)}), bf16[32,8,768]{2,1,0:T(8,128)(2,1)S(1)}, u32[]{:S(2)}, u32[]{:S(2)}) %all-to-all-start) | async-done | bytes 393248 | tf_op jit(solution)/shard_map/all_to_all | solution.py:354
  31.1 3.0 %collective-permute-start.5 = (bf16[2,192,256]{2,1,0:T(8,128)(2,1)}, bf16[2,192,256]{2,1,0:T(8,128)(2,1)S(1)}, u32[]{:S(2)}, u32[]{:S(2)}) collective-permute-start(bf16[2,192,256]{2,1,0:T(8,128)(2,1)} %get-tuple-element.30), channel_id=1, source_target_pairs={{0,4},{1,5},{2,6},{3,7},{4,0},{5,1},{6,2},{7,3},{8,12},{9,13},{10,... | collective-permute-start | bytes 589832 | tf_op jit(solution)/shard_map/ppermute | solution.py:375
  34.7 1.5 %copy-done.1 = bf16[2,576,768]{2,1,0:T(8,128)(2,1)S(1)} copy-done((bf16[2,576,768]{2,1,0:T(8,128)(2,1)S(1)}, bf16[2,576,768]{2,1,0:T(8,128)(2,1)}, u32[]{:S(2)}) %copy-start.1) | copy-done | bytes 1769496
  37.6 2.7 %collective-permute-start = (bf16[2,192,256]{2,1,0:T(8,128)(2,1)S(1)}, bf16[2,192,256]{2,1,0:T(8,128)(2,1)S(1)}, u32[]{:S(2)}, u32[]{:S(2)}) collective-permute-start(bf16[2,192,256]{2,1,0:T(8,128)(2,1)S(1)} %get-tuple-element.23), channel_id=1, source_target_pairs={{0,6},{1,7},{2,0},{3,1},{4,2},{5,3},{6,4},{7,5},{8,14},{9,15},{10,... | collective-permute-start | bytes 589832 | tf_op jit(solution)/shard_map/ppermute | solution.py:375
  41.0 1.3 collective-permute-done.6.refs_3_
  43.4 3.1 %prep_left.1.refs_4_ = bf16[2,1536,768]{2,1,0:T(8,128)(2,1)S(1)} custom-call(s32[8]{0:T(128)S(1)} %fusion.5.place_ref, bf16[1,2,16,96,2,384]{5,4,3,2,1,0:T(2,128)(2,1)S(1)} %copy-done.4), custom_call_target="tpu_custom_call" | custom-call | bytes 14155776 | tf_op jit(solution)/shard_map/prep_left/pallas_call | solution.py:359
  46.5 1.7 %reply.4.refs_5_ = f32[2,256,768]{2,1,0:T(8,128)S(1)} custom-call(bf16[2,192,256]{2,1,0:T(8,128)(2,1)S(1)} %get-tuple-element.28.refs_0_, bf16[2,192,256]{2,1,0:T(8,128)(2,1)S(1)} %collective-permute-done.4.refs_1_, bf16[2,192,256]{2,1,0:T(8,128)(2,1)S(1)} %collective-permute-done.5.refs_2_, bf16[2,192,256]{2,1,0:T(8,128)(2,1)} %collective-permute-done.6.refs_3_, ...), custom_call_target="tpu_custom_call" | custom-call | flops 603979776 | bytes 2359296 | tf_op jit(solution)/shard_map/reply/pallas_call | solution.py:338
  48.3 1.5 %collective-permute-done.refs_0_ = bf16[2,192,256]{2,1,0:T(8,128)(2,1)S(1)} collective-permute-done((bf16[2,192,256]{2,1,0:T(8,128)(2,1)S(1)}, bf16[2,192,256]{2,1,0:T(8,128)(2,1)S(1)}, u32[]{:S(2)}, u32[]{:S(2)}) %collective-permute-start) | collective-permute-done | bytes 196640 | tf_op jit(solution)/shard_map/ppermute | solution.py:375
  49.7 2.9 %collective-permute-done.2.refs_2_ = bf16[2,192,256]{2,1,0:T(8,128)(2,1)S(1)} collective-permute-done((bf16[2,192,256]{2,1,0:T(8,128)(2,1)S(1)}, bf16[2,192,256]{2,1,0:T(8,128)(2,1)S(1)}, u32[]{:S(2)}, u32[]{:S(2)}) %collective-permute-start.2) | collective-permute-done | bytes 196640 | tf_op jit(solution)/shard_map/ppermute | solution.py:375
  54.5 19.3 %all_to_all.20 = bf16[32,8,768]{2,1,0:T(8,128)(2,1)S(1)} all-to-all(bf16[32,8,768]{2,1,0:T(8,128)(2,1)S(1)} %bitcast.16), channel_id=1, replica_groups=mesh['freq'=32,'tcol'=4,'trow'=2] {'freq'}, dimensions={0} | all-to-all | bytes 786432 | tf_op jit(solution)/shard_map/all_to_all | solution.py:386
  73.8 2.3 %middle.1 = (bf16[4,768,256]{2,1,0:T(8,128)(2,1)}, bf16[256,768]{1,0:T(8,128)(2,1)S(1)}) custom-call(bf16[256,256]{1,0:T(8,128)(2,1)S(1)} %copy-done.5, s32[4,768]{1,0:T(4,128)S(1)} %copy-done.6, bf16[256,768]{1,0:T(8,128)(2,1)S(1)} %bitcast.17), custom_call_target="tpu_custom_call" | custom-call | tf_op jit(solution)/shard_map/middle/pallas_call | solution.py:391
  76.2 19.0 %all_to_all.21 = bf16[32,8,768]{2,1,0:T(8,128)(2,1)S(1)} all-to-all(bf16[32,8,768]{2,1,0:T(8,128)(2,1)S(1)} %bitcast.19), channel_id=1, replica_groups=mesh['freq'=32,'tcol'=4,'trow'=2] {'freq'}, dimensions={0} | all-to-all | bytes 786432 | tf_op jit(solution)/shard_map/all_to_all | solution.py:354
  95.7 3.0 %collective-permute-start.12 = (bf16[2,192,256]{2,1,0:T(8,128)(2,1)S(1)}, bf16[2,192,256]{2,1,0:T(8,128)(2,1)S(1)}, u32[]{:S(2)}, u32[]{:S(2)}) collective-permute-start(bf16[2,192,256]{2,1,0:T(8,128)(2,1)S(1)} %get-tuple-element.40), channel_id=1, source_target_pairs={{0,4},{1,5},{2,6},{3,7},{4,0},{5,1},{6,2},{7,3},{8,12},{9,13},{10,... | collective-permute-start | bytes 589832 | tf_op jit(solution)/shard_map/ppermute | solution.py:375
  98.7 2.2 %collective-permute-start.13 = (bf16[2,192,256]{2,1,0:T(8,128)(2,1)S(1)}, bf16[2,192,256]{2,1,0:T(8,128)(2,1)S(1)}, u32[]{:S(2)}, u32[]{:S(2)}) collective-permute-start(bf16[2,192,256]{2,1,0:T(8,128)(2,1)S(1)} %get-tuple-element.41), channel_id=1, source_target_pairs={{0,2},{1,3},{2,4},{3,5},{4,6},{5,7},{6,0},{7,1},{8,10},{9,11},{10,... | collective-permute-start | bytes 589832 | tf_op jit(solution)/shard_map/ppermute | solution.py:375
  104.7 1.3 collective-permute-start.8
  106.4 1.4 collective-permute-start.9
  108.6 5.1 %collective-permute-done.7.refs_0_ = bf16[2,192,256]{2,1,0:T(8,128)(2,1)S(1)} collective-permute-done((bf16[2,192,256]{2,1,0:T(8,128)(2,1)S(1)}, bf16[2,192,256]{2,1,0:T(8,128)(2,1)S(1)}, u32[]{:S(2)}, u32[]{:S(2)}) %collective-permute-start.7) | collective-permute-done | bytes 196640 | tf_op jit(solution)/shard_map/ppermute | solution.py:375
  113.8 3.5 %collective-permute-done.9.refs_2_ = bf16[2,192,256]{2,1,0:T(8,128)(2,1)S(1)} collective-permute-done((bf16[2,192,256]{2,1,0:T(8,128)(2,1)S(1)}, bf16[2,192,256]{2,1,0:T(8,128)(2,1)S(1)}, u32[]{:S(2)}, u32[]{:S(2)}) %collective-permute-start.9) | collective-permute-done | bytes 196640 | tf_op jit(solution)/shard_map/ppermute | solution.py:375
  118.1 20.2 %all_to_all.22 = bf16[32,8,768]{2,1,0:T(8,128)(2,1)S(1)} all-to-all(bf16[32,8,768]{2,1,0:T(8,128)(2,1)S(1)} %bitcast.15), channel_id=1, replica_groups=mesh['freq'=32,'tcol'=4,'trow'=2] {'freq'}, dimensions={0} | all-to-all | bytes 786432 | tf_op jit(solution)/shard_map/all_to_all | solution.py:386
  138.3 1.6 %last.1 = bf16[4,768,256]{2,1,0:T(8,128)(2,1)} custom-call(bf16[256,256]{1,0:T(8,128)(2,1)S(1)} %copy-done.5, s32[4,768]{1,0:T(4,128)S(1)} %copy-done.6, bf16[256,768]{1,0:T(8,128)(2,1)S(1)} %bitcast.18), custom_call_target="tpu_custom_call" | custom-call | tf_op jit(solution)/shard_map/last/pallas_call | solution.py:400
  (51 shorter events, 14.5 us)
Async XLA Ops:
  0.6 14.5 %copy-start.10 = (s32[8]{0:T(128)S(1)}, s32[8]{0:T(128)}, u32[]{:S(2)}) copy-start(s32[8]{0:T(128)} %constant.41.clone) | copy-start | bytes 100
  0.6 14.5 %copy-start.11 = (s32[8]{0:T(128)S(1)}, s32[8]{0:T(128)}, u32[]{:S(2)}) copy-start(s32[8]{0:T(128)} %constant.42.clone) | copy-start | bytes 100
  0.7 14.4 %copy-start.7 = (s32[1,16,2]{1,2,0:T(2,128)S(1)}, s32[1,16,2]{1,2,0:T(2,128)}, u32[]{:S(2)}) copy-start(s32[1,16,2]{1,2,0:T(2,128)} %param.12) | copy-start | bytes 388
  3.6 26.3 %all-to-all-start = ((bf16[32,8,768]{2,1,0:T(8,128)(2,1)}), bf16[32,8,768]{2,1,0:T(8,128)(2,1)S(1)}, u32[]{:S(2)}, u32[]{:S(2)}) async-start(bf16[32,8,768]{2,1,0:T(8,128)(2,1)} %bitcast.20), calls=%async_computation | async-start | bytes 786432 | tf_op jit(solution)/shard_map/all_to_all | solution.py:354
  31.1 9.3 %collective-permute-start.5 = (bf16[2,192,256]{2,1,0:T(8,128)(2,1)}, bf16[2,192,256]{2,1,0:T(8,128)(2,1)S(1)}, u32[]{:S(2)}, u32[]{:S(2)}) collective-permute-start(bf16[2,192,256]{2,1,0:T(8,128)(2,1)} %get-tuple-element.30), channel_id=1, source_target_pairs={{0,4},{1,5},{2,6},{3,7},{4,0},{5,1},{6,2},{7,3},{8,12},{9,13},{10,... | collective-permute-start | bytes 589832 | tf_op jit(solution)/shard_map/ppermute | solution.py:375
  34.1 8.2 %collective-permute-start.6 = (bf16[2,192,256]{2,1,0:T(8,128)(2,1)}, bf16[2,192,256]{2,1,0:T(8,128)(2,1)}, u32[]{:S(2)}, u32[]{:S(2)}) collective-permute-start(bf16[2,192,256]{2,1,0:T(8,128)(2,1)} %get-tuple-element.31), channel_id=1, source_target_pairs={{0,2},{1,3},{2,4},{3,5},{4,6},{5,7},{6,0},{7,1},{8,10},{9,11},{10,... | collective-permute-start | bytes 589832 | tf_op jit(solution)/shard_map/ppermute | solution.py:375
  36.2 7.2 %copy-start.4 = (bf16[1,2,16,96,2,384]{5,4,3,2,1,0:T(2,128)(2,1)S(1)}, bf16[1,2,16,96,2,384]{5,4,3,2,1,0:T(2,128)(2,1)}, u32[]{:S(2)}) copy-start(bf16[1,2,16,96,2,384]{5,4,3,2,1,0:T(2,128)(2,1)} %factor_ref.3) | copy-start | bytes 14155780
  36.8 6.5 %copy-start.8 = (s32[8]{0:T(128)S(1)}, s32[8]{0:T(128)}, u32[]{:S(2)}) copy-start(s32[8]{0:T(128)} %constant.43.clone) | copy-start | bytes 100
  36.9 6.5 %copy-start.9 = (s32[8]{0:T(128)S(1)}, s32[8]{0:T(128)}, u32[]{:S(2)}) copy-start(s32[8]{0:T(128)} %constant.51) | copy-start | bytes 100
  36.9 9.6 %collective-permute-start.4 = (bf16[2,192,256]{2,1,0:T(8,128)(2,1)S(1)}, bf16[2,192,256]{2,1,0:T(8,128)(2,1)S(1)}, u32[]{:S(2)}, u32[]{:S(2)}) collective-permute-start(bf16[2,192,256]{2,1,0:T(8,128)(2,1)S(1)} %get-tuple-element.29), channel_id=1, source_target_pairs={{0,1},{1,0},{2,3},{3,2},{4,5},{5,4},{6,7},{7,6},{8,9},{9,8},{10,11... | collective-permute-start | bytes 589832 | tf_op jit(solution)/shard_map/ppermute | solution.py:375
  37.6 12.1 %collective-permute-start = (bf16[2,192,256]{2,1,0:T(8,128)(2,1)S(1)}, bf16[2,192,256]{2,1,0:T(8,128)(2,1)S(1)}, u32[]{:S(2)}, u32[]{:S(2)}) collective-permute-start(bf16[2,192,256]{2,1,0:T(8,128)(2,1)S(1)} %get-tuple-element.23), channel_id=1, source_target_pairs={{0,6},{1,7},{2,0},{3,1},{4,2},{5,3},{6,4},{7,5},{8,14},{9,15},{10,... | collective-permute-start | bytes 589832 | tf_op jit(solution)/shard_map/ppermute | solution.py:375
  40.4 9.4 %collective-permute-start.1 = (bf16[2,192,256]{2,1,0:T(8,128)(2,1)S(1)}, bf16[2,192,256]{2,1,0:T(8,128)(2,1)S(1)}, u32[]{:S(2)}, u32[]{:S(2)}) collective-permute-start(bf16[2,192,256]{2,1,0:T(8,128)(2,1)S(1)} %get-tuple-element.24), channel_id=1, source_target_pairs={{0,5},{1,4},{2,7},{3,6},{4,1},{5,0},{6,3},{7,2},{8,13},{9,12},{10,... | collective-permute-start | bytes 589832 | tf_op jit(solution)/shard_map/ppermute | solution.py:375
  40.4 12.2 %collective-permute-start.2 = (bf16[2,192,256]{2,1,0:T(8,128)(2,1)S(1)}, bf16[2,192,256]{2,1,0:T(8,128)(2,1)S(1)}, u32[]{:S(2)}, u32[]{:S(2)}) collective-permute-start(bf16[2,192,256]{2,1,0:T(8,128)(2,1)S(1)} %get-tuple-element.25), channel_id=1, source_target_pairs={{0,3},{1,2},{2,5},{3,4},{4,7},{5,6},{6,1},{7,0},{8,11},{9,10},{10,... | collective-permute-start | bytes 589832 | tf_op jit(solution)/shard_map/ppermute | solution.py:375
  42.3 11.3 %collective-permute-start.3 = (bf16[2,192,256]{2,1,0:T(8,128)(2,1)S(1)}, bf16[2,192,256]{2,1,0:T(8,128)(2,1)S(1)}, u32[]{:S(2)}, u32[]{:S(2)}) collective-permute-start(bf16[2,192,256]{2,1,0:T(8,128)(2,1)S(1)} %get-tuple-element.27), channel_id=1, source_target_pairs={{0,7},{1,6},{2,1},{3,0},{4,3},{5,2},{6,5},{7,4},{8,15},{9,14},{10,... | collective-permute-start | bytes 589832 | tf_op jit(solution)/shard_map/ppermute | solution.py:375
  48.2 25.6 %copy-start.5 = (bf16[256,256]{1,0:T(8,128)(2,1)S(1)}, bf16[256,256]{1,0:T(8,128)(2,1)}, u32[]{:S(2)}) copy-start(bf16[256,256]{1,0:T(8,128)(2,1)} %constant.50.table_hbm.table_ref) | copy-start | bytes 393220
  48.2 25.6 %copy-start.6 = (s32[4,768]{1,0:T(4,128)S(1)}, s32[4,768]{1,0:T(4,128)}, u32[]{:S(2)}) copy-start(s32[4,768]{1,0:T(4,128)} %window_ref.3) | copy-start | bytes 36868
  95.1 5.8 %copy-start.2 = (bf16[2,576,768]{2,1,0:T(8,128)(2,1)S(1)}, bf16[2,576,768]{2,1,0:T(8,128)(2,1)}, u32[]{:S(2)}) copy-start(bf16[2,576,768]{2,1,0:T(8,128)(2,1)} %copy-done) | copy-start | bytes 5308420
  95.7 9.0 %collective-permute-start.12 = (bf16[2,192,256]{2,1,0:T(8,128)(2,1)S(1)}, bf16[2,192,256]{2,1,0:T(8,128)(2,1)S(1)}, u32[]{:S(2)}, u32[]{:S(2)}) collective-permute-start(bf16[2,192,256]{2,1,0:T(8,128)(2,1)S(1)} %get-tuple-element.40), channel_id=1, source_target_pairs={{0,4},{1,5},{2,6},{3,7},{4,0},{5,1},{6,2},{7,3},{8,12},{9,13},{10,... | collective-permute-start | bytes 589832 | tf_op jit(solution)/shard_map/ppermute | solution.py:375
  98.7 7.8 %collective-permute-start.13 = (bf16[2,192,256]{2,1,0:T(8,128)(2,1)S(1)}, bf16[2,192,256]{2,1,0:T(8,128)(2,1)S(1)}, u32[]{:S(2)}, u32[]{:S(2)}) collective-permute-start(bf16[2,192,256]{2,1,0:T(8,128)(2,1)S(1)} %get-tuple-element.41), channel_id=1, source_target_pairs={{0,2},{1,3},{2,4},{3,5},{4,6},{5,7},{6,0},{7,1},{8,10},{9,11},{10,... | collective-permute-start | bytes 589832 | tf_op jit(solution)/shard_map/ppermute | solution.py:375
  101.6 6.3 %collective-permute-start.11 = (bf16[2,192,256]{2,1,0:T(8,128)(2,1)S(1)}, bf16[2,192,256]{2,1,0:T(8,128)(2,1)S(1)}, u32[]{:S(2)}, u32[]{:S(2)}) collective-permute-start(bf16[2,192,256]{2,1,0:T(8,128)(2,1)S(1)} %get-tuple-element.39), channel_id=1, source_target_pairs={{0,1},{1,0},{2,3},{3,2},{4,5},{5,4},{6,7},{7,6},{8,9},{9,8},{10,11... | collective-permute-start | bytes 589832 | tf_op jit(solution)/shard_map/ppermute | solution.py:375
  101.7 7.0 %collective-permute-start.10 = (bf16[2,192,256]{2,1,0:T(8,128)(2,1)S(1)}, bf16[2,192,256]{2,1,0:T(8,128)(2,1)S(1)}, u32[]{:S(2)}, u32[]{:S(2)}) collective-permute-start(bf16[2,192,256]{2,1,0:T(8,128)(2,1)S(1)} %get-tuple-element.37), channel_id=1, source_target_pairs={{0,7},{1,6},{2,1},{3,0},{4,3},{5,2},{6,5},{7,4},{8,15},{9,14},{10,... | collective-permute-start | bytes 589832 | tf_op jit(solution)/shard_map/ppermute | solution.py:375
  103.4 10.3 %collective-permute-start.7 = (bf16[2,192,256]{2,1,0:T(8,128)(2,1)S(1)}, bf16[2,192,256]{2,1,0:T(8,128)(2,1)S(1)}, u32[]{:S(2)}, u32[]{:S(2)}) collective-permute-start(bf16[2,192,256]{2,1,0:T(8,128)(2,1)S(1)} %get-tuple-element.34), channel_id=1, source_target_pairs={{0,6},{1,7},{2,0},{3,1},{4,2},{5,3},{6,4},{7,5},{8,14},{9,15},{10,... | collective-permute-start | bytes 589832 | tf_op jit(solution)/shard_map/ppermute | solution.py:375
  104.7 9.0 %collective-permute-start.8 = (bf16[2,192,256]{2,1,0:T(8,128)(2,1)S(1)}, bf16[2,192,256]{2,1,0:T(8,128)(2,1)S(1)}, u32[]{:S(2)}, u32[]{:S(2)}) collective-permute-start(bf16[2,192,256]{2,1,0:T(8,128)(2,1)S(1)} %get-tuple-element.35), channel_id=1, source_target_pairs={{0,5},{1,4},{2,7},{3,6},{4,1},{5,0},{6,3},{7,2},{8,13},{9,12},{10,... | collective-permute-start | bytes 589832 | tf_op jit(solution)/shard_map/ppermute | solution.py:375
  106.4 10.8 %collective-permute-start.9 = (bf16[2,192,256]{2,1,0:T(8,128)(2,1)S(1)}, bf16[2,192,256]{2,1,0:T(8,128)(2,1)S(1)}, u32[]{:S(2)}, u32[]{:S(2)}) collective-permute-start(bf16[2,192,256]{2,1,0:T(8,128)(2,1)S(1)} %get-tuple-element.36), channel_id=1, source_target_pairs={{0,3},{1,2},{2,5},{3,4},{4,7},{5,6},{6,1},{7,0},{8,11},{9,10},{10,... | collective-permute-start | bytes 589832 | tf_op jit(solution)/shard_map/ppermute | solution.py:375
  (3 other events, 5.1 us)

commit v3 on v2

--- a/solution.py
+++ b/solution.py
@@ -11,11 +11,11 @@
 
 
 MIB = 1 << 20
-PARTNERS = ((2, 0), (1, 0), (3, 0), (2, 1), (1, 1), (3, 1), (0, 1), (0, 0))
+LANES = 128
+PARTNERS = ((2, 0), (2, 1), (1, 0), (3, 0), (1, 1), (3, 1), (0, 1), (0, 0))
 SPLIT = 5
-CALLS = ((0, 2), (2, 5), (5, 8))
-EARLY = (7, 6, 0, 1)
-LATE = (2, 3, 4, 5)
+CALLS = ((0, 1), (1, 5), (5, 8))
+REPLIES = ((7, 6, 0, 1, 2), (3, 4, 5))
 
 
 def spectral_rows(count_freq, time_len, repeat):
@@ -61,14 +61,15 @@
     return padded.T
 
 
-def mute(block, window):
-    rows, length = block.shape
-    lanes = 128
-    limit = jnp.broadcast_to(window, (rows, lanes)).astype(jnp.bfloat16)
+def lane_limits(window):
+    return jnp.broadcast_to(window, (window.shape[0], LANES)).astype(jnp.bfloat16)
+
+
+def mute(block, limit):
     kept = []
-    for start in range(0, length, lanes):
-        at = lax.broadcasted_iota(jnp.int32, (rows, lanes), 1) + start
-        part = block[:, start : start + lanes]
+    for start in range(0, block.shape[1], LANES):
+        at = lax.broadcasted_iota(jnp.int32, limit.shape, 1) + start
+        part = block[:, start : start + LANES]
         kept.append(jnp.where(at.astype(jnp.bfloat16) < limit, part, jnp.zeros_like(part)))
     return jnp.concatenate(kept, axis=1)
 
@@ -77,19 +78,18 @@
     return nt_dot(table, jnp.concatenate(signals, axis=1)).astype(jnp.bfloat16)
 
 
-def to_time(table, replies, window, points):
+def to_time(table, replies, limits):
     waves = tn_dot(replies, table).astype(jnp.bfloat16)
+    points = len(limits)
     length = waves.shape[1] // points
-    return [
-        mute(waves[:, p * length : (p + 1) * length], window[:, p : p + 1])
-        for p in range(points)
-    ]
+    return [mute(waves[:, p * length : (p + 1) * length], limits[p]) for p in range(points)]
 
 
 def first_kernel(
     scale, step, table_hbm, window_hbm, field_hbm, out_ref, table_ref, window_ref, field_ref, sems
 ):
     points, src_rows, _ = field_ref.shape
+    chunks = src_rows // step
     small = [
         pltpu.make_async_copy(window_hbm, window_ref, sems.at[points]),
         pltpu.make_async_copy(table_hbm, table_ref, sems.at[points + 1]),
@@ -102,50 +102,80 @@
         copy.start()
     small[0].wait()
     window = stand_window(window_ref[...])
+    limits = [lane_limits(window[:, point : point + 1]) for point in range(points)]
     small[1].wait()
     table = spread_table(table_ref[...], points, scale)
     for copy in copies:
         copy.wait()
+    for number in range(chunks):
+        part = slice(number * step, (number + 1) * step)
+        signals = [mute(field_ref[point, part], limits[point][part]) for point in range(points)]
+        out_ref[:, part] = to_freq(table, signals)
+
+
+def tables_kernel(
+    back_scale, scale, table_ref, window_ref, back_ref, turned_ref, forth_ref, limit_ref
+):
+    points = limit_ref.shape[0]
+    table = table_ref[...]
+    back = spread_table(table, points, back_scale)
+    back_ref[...] = back
+    turned_ref[...] = back.astype(jnp.float32).T.astype(jnp.bfloat16)
+    forth_ref[...] = spread_table(table, points, scale)
+    window = stand_window(window_ref[...])
+    for point in range(points):
+        limit_ref[point] = lane_limits(window[:, point : point + 1])
+
+
+def middle_kernel(step, turned_ref, forth_ref, window_ref, reply_ref, pass_ref, out_ref):
+    points, length, src_rows = pass_ref.shape
     for start in range(0, src_rows, step):
-        signals = [
-            mute(
-                field_ref[point, start : start + step],
-                window[start : start + step, point : point + 1],
-            )
-            for point in range(points)
-        ]
-        out_ref[:, start : start + step] = to_freq(table, signals)
-
-
-def middle_kernel(back_scale, scale, step, table_ref, window_ref, reply_ref, pass_ref, out_ref):
+        part = slice(start, start + step)
+        waves = jnp.dot(
+            turned_ref[...], reply_ref[:, part], preferred_element_type=jnp.float32
+        ).astype(jnp.bfloat16)
+        at = lax.broadcasted_iota(jnp.int32, (length, step), 0).astype(jnp.bfloat16)
+        kept = []
+        for point in range(points):
+            limit = window_ref[point : point + 1, part].astype(jnp.float32)
+            limit = jnp.broadcast_to(limit, (length, step)).astype(jnp.bfloat16)
+            block = waves[point * length : (point + 1) * length]
+            kept.append(jnp.where(at < limit, block, jnp.zeros_like(block)))
+            pass_ref[point, :, part] = kept[-1]
+        signal = jnp.concatenate(kept, axis=0)
+        out_ref[:, part] = jnp.dot(
+            forth_ref[...], signal, preferred_element_type=jnp.float32
+        ).astype(jnp.bfloat16)
+
+
+def store_kernel(step, turned_ref, pass_hbm, pass_ref, sems):
     points, src_rows, _ = pass_ref.shape
-    back = spread_table(table_ref[...], points, back_scale)
-    table = spread_table(table_ref[...], points, scale)
-    window = stand_window(window_ref[...])
-    for start in range(0, src_rows, step):
-        blocks = to_time(
-            back, reply_ref[:, start : start + step], window[start : start + step], points
+    copies = []
+    for point in range(points):
+        for start in range(0, src_rows, step):
+            block = turned_ref[point, :, start : start + step].astype(jnp.float32)
+            pass_ref[point, start : start + step] = block.T.astype(jnp.bfloat16)
+        copies.append(
+            pltpu.make_async_copy(pass_ref.at[point], pass_hbm.at[point], sems.at[point])
         )
-        for point in range(points):
-            pass_ref[point, start : start + step] = blocks[point]
-        out_ref[:, start : start + step] = to_freq(table, blocks)
-
-
-def last_kernel(back_scale, step, table_ref, window_ref, reply_ref, pass_hbm, pass_ref, sems):
+        copies[-1].start()
+    for copy in copies:
+        copy.wait()
+
+
+def last_kernel(step, back_ref, limit_ref, reply_ref, pass_hbm, pass_ref, sems):
     points, src_rows, _ = pass_ref.shape
-    table = spread_table(table_ref[...], points, back_scale)
-    window = stand_window(window_ref[...])
     copies = []
     for number, start in enumerate(range(0, src_rows, step)):
-        part = pl.ds(start, step)
-        blocks = to_time(
-            table, reply_ref[:, start : start + step], window[start : start + step], points
-        )
+        part = slice(start, start + step)
+        limits = [limit_ref[point, part] for point in range(points)]
+        blocks = to_time(back_ref[...], reply_ref[:, part], limits)
         for point in range(points):
-            pass_ref[point, start : start + step] = blocks[point]
+            pass_ref[point, part] = blocks[point]
             copies.append(
                 pltpu.make_async_copy(
-                    pass_ref.at[point, part, :], pass_hbm.at[point, part, :],
+                    pass_ref.at[point, pl.ds(start, step), :],
+                    pass_hbm.at[point, pl.ds(start, step), :],
                     sems.at[number, point],
                 )
             )
@@ -222,23 +252,18 @@
                 ]
 
 
-def reply_sum(first, coef_refs, left_ref, tile):
-    depth = coef_refs[0].shape[1]
-    coef = jnp.concatenate([ref[tile] for ref in coef_refs], axis=0)
-    return tn_dot(coef, left_ref[tile, first * depth : (first + len(coef_refs)) * depth])
-
-
-def early_kernel(*refs):
-    *coef_refs, left_ref, out_ref = refs
-    for tile in range(out_ref.shape[0]):
-        out_ref[tile] = reply_sum(0, coef_refs, left_ref, tile)
-
-
-def late_kernel(sign, half, *refs):
-    *coef_refs, left_ref, sum_ref, out_ref = refs
-    tile_len = sum_ref.shape[2] // 2
-    for tile in range(sum_ref.shape[0]):
-        both = reply_sum(len(EARLY), coef_refs, left_ref, tile) + sum_ref[tile]
+def reply_kernel(sign, half, first, count, starts, ends, *refs):
+    coef_refs, left_ref, out_ref = refs[:count], refs[count], refs[-1]
+    row_tiles, depth, _ = coef_refs[0].shape
+    tile_len = left_ref.shape[2] // 2
+    for tile in range(row_tiles):
+        coef = jnp.concatenate([ref[tile] for ref in coef_refs], axis=0)
+        both = tn_dot(coef, left_ref[tile, first * depth : (first + count) * depth])
+        if not starts:
+            both = both + refs[count + 1][tile]
+        if not ends:
+            out_ref[tile] = both
+            continue
         other = both[:, tile_len:]
         other = swap_parts(other, half) * part_sign(other.shape, half, -sign)
         reply = both[:, :tile_len] + other
@@ -267,6 +292,7 @@
     params = pltpu.CompilerParams(vmem_limit_bytes=24 * MIB)
     rows_shape = jax.ShapeDtypeStruct((rows, src_rows), bf16)
     pass_shape = jax.ShapeDtypeStruct(focal_field.shape, bf16)
+    sums_shape = jax.ShapeDtypeStruct((row_tiles, rows, parts_two * tile_len), jnp.float32)
 
     def cost(flops, moved):
         return pl.CostEstimate(flops=flops, bytes_accessed=moved, transcendentals=0)
@@ -276,7 +302,7 @@
     chip, core = lax.axis_index("tcol"), lax.axis_index("trow")
     core_at = jnp.bitwise_xor(core, other_core)
     targets = (chip + steps) % chips * cores + core_at
-    order = np.array(EARLY + LATE)
+    order = np.array(sum(REPLIES, ()))
     arriving = jnp.bitwise_xor(core, other_core[order])
     sources = (chip + chips - steps[order]) % chips * cores + arriving
     pairs = []
@@ -334,22 +360,26 @@
             name="coef",
         )(moved, factors)
 
-    def reply_call(kernel, count, out_shape, operands):
+    def reply_call(sign, arrived, call, total):
+        slots = REPLIES[call]
+        first = sum(len(group) for group in REPLIES[:call])
+        ends = call == len(REPLIES) - 1
+        operands = [arrived[slot] for slot in slots] + [left] + ([] if call == 0 else [total])
         return pl.pallas_call(
-            kernel,
+            functools.partial(
+                reply_kernel, sign, points, first, len(slots), call == 0, ends
+            ),
             in_specs=[whole] * len(operands),
             out_specs=whole,
-            out_shape=out_shape,
+            out_shape=rows_shape if ends else sums_shape,
             compiler_params=params,
             cost_estimate=cost(
-                2 * count * row_tiles * depth * parts_two * tile_len * rows,
-                count * factor_size // 4,
+                2 * len(slots) * row_tiles * depth * parts_two * tile_len * rows,
+                len(slots) * factor_size // 4,
             ),
             name="reply",
         )(*operands)
 
-    outputs = []
-    outputs = []
     for number, sign in enumerate((1.0, -1.0)):
         moved = lax.all_to_all(
             spectrum.reshape(freqs, 2 * points, src_rows), "freq",
@@ -367,6 +397,31 @@
                 cost_estimate=cost(0, 6 * factor_size),
                 name="prep_left",
             )(sources, left_factors)
+            tables = pl.pallas_call(
+                functools.partial(tables_kernel, back_scale, scale),
+                in_specs=[whole, whole],
+                out_specs=[whole] * 4,
+                out_shape=[
+                    jax.ShapeDtypeStruct((rows, points * time_len), bf16),
+                    jax.ShapeDtypeStruct((points * time_len, rows), bf16),
+                    jax.ShapeDtypeStruct((rows, points * time_len), bf16),
+                    jax.ShapeDtypeStruct((points, src_rows, LANES), bf16),
+                ],
+                compiler_params=params,
+                cost_estimate=cost(0, 4 * points * src_rows * LANES),
+                name="tables",
+            )(table, mute_window)
+        if number == 1:
+            first = pl.pallas_call(
+                functools.partial(store_kernel, step),
+                in_specs=[whole],
+                out_specs=anywhere,
+                out_shape=pass_shape,
+                scratch_shapes=[pltpu.VMEM(pass_shape.shape, bf16), dma((points,))],
+                compiler_params=params,
+                cost_estimate=cost(0, 6 * points * src_rows * time_len),
+                name="store",
+            )(turned)
         blocks = []
         for begin, end in CALLS:
             blocks += coefficients(sign, moved, begin, end)
@@ -374,40 +429,33 @@
         for slot, pair in enumerate(pairs):
             arrived.append(lax.ppermute(blocks[slot], ("tcol", "trow"), pair))
         arrived.append(blocks[-1])
-        part = reply_call(
-            early_kernel, len(EARLY),
-            jax.ShapeDtypeStruct((row_tiles, rows, parts_two * tile_len), jnp.float32),
-            [arrived[slot] for slot in EARLY] + [left],
-        )
-        replies = reply_call(
-            functools.partial(late_kernel, sign, points), len(LATE), rows_shape,
-            [arrived[slot] for slot in LATE] + [left, part],
-        )
+        replies = None
+        for call in range(len(REPLIES)):
+            replies = reply_call(sign, arrived, call, replies)
         replies = lax.all_to_all(
             replies.reshape(freqs, 2 * points, src_rows), "freq",
             split_axis=0, concat_axis=0, tiled=True,
         ).reshape(rows, src_rows)
         if number == 0:
-            done, spectrum = pl.pallas_call(
-                functools.partial(middle_kernel, back_scale, scale, step),
-                in_specs=[whole, whole, whole],
+            turned, spectrum = pl.pallas_call(
+                functools.partial(middle_kernel, step),
+                in_specs=[whole] * 4,
                 out_specs=(whole, whole),
-                out_shape=(pass_shape, rows_shape),
+                out_shape=(jax.ShapeDtypeStruct((points, time_len, src_rows), bf16), rows_shape),
                 compiler_params=params,
                 name="middle",
-            )(table, mute_window, replies)
+            )(tables[1], tables[2], mute_window, replies)
         else:
-            done = pl.pallas_call(
-                functools.partial(last_kernel, back_scale, step),
+            second = pl.pallas_call(
+                functools.partial(last_kernel, step),
                 in_specs=[whole, whole, whole],
                 out_specs=anywhere,
                 out_shape=pass_shape,
                 scratch_shapes=[pltpu.VMEM(pass_shape.shape, bf16), dma((chunks, points))],
                 compiler_params=params,
                 name="last",
-            )(table, mute_window, replies)
-        outputs.append(done)
-    return (outputs[0], outputs[1])
+            )(tables[0], tables[3], replies)
+    return (first, second)
 
 
 def solution(mesh):

time: 140 us -> 146 us (1.043); the launches traced: 140 us -> 144 us
  blocking collectives: 58.5 us -> 19.6 us
  waiting for transfers between devices: 21.5 us -> 46.7 us
  local copies, waits for them, and re-layouts: 5.17 us -> 13.4 us
  starting transfers between devices: 29.6 us -> 36.5 us
  Pallas kernels: 24.1 us -> 26.8 us
    all_to_all x2 -> x0, blocking collectives: 39.5 us -> none  [body(): lax.all_to_all(replies.reshape(freqs, 2 * points, src_rows), 'freq', spli...]
    all_to_all x0 -> x2, waiting for transfers between devices: none -> 25.7 us  [body(): lax.all_to_all(replies.reshape(freqs, 2 * points, src_rows), 'freq', spli...]
    all_to_all x0 -> x2, starting transfers between devices: none -> 9.47 us  [body(): lax.all_to_all(replies.reshape(freqs, 2 * points, src_rows), 'freq', spli...]
    unnamed x24 -> x58, local copies, waits for them, and re-layouts: 5.09 us -> 13.4 us
    pallas_call x6 -> x8, Pallas kernels: 8.13 us -> 10.9 us  [the longest x4 6.29 us: reply_call(): pl.pallas_call(functools.partial(reply_kernel, sign, points, first, len(s...]
    ppermute x14, starting transfers between devices: 18.2 us -> 15.7 us  [body(): arrived.append(lax.ppermute(blocks[slot], ('tcol', 'trow'), pair))]
  transfers between devices with their start and end apart: 15 -> 17, of which waited for: 9 -> 12; matrix products, arithmetic and copies ran while one was open for 0% -> 0% of each run, Pallas kernels for 10% -> 11%
where the time goes in v3:
time: 146 us; the launch traced here: 144 us
  waiting for transfers between devices  46.7 us (32%)
  starting transfers between devices  36.5 us (25%)
  Pallas kernels  26.8 us (18%)
  blocking collectives  19.6 us (13%)
  local copies, waits for them, and re-layouts  13.4 us (9%)
    all_to_all x2, waiting for transfers between devices, body(): lax.all_to_all(replies.reshape(freqs, 2 * points, src_rows), 'freq', spli...  25.7 us
    all_to_all x1, blocking collectives, body(): lax.all_to_all(spectrum.reshape(freqs, 2 * points, src_rows), 'freq', spl...  19.6 us
    ppermute x14, starting transfers between devices, body(): arrived.append(lax.ppermute(blocks[slot], ('tcol', 'trow'), pair))  15.7 us
    ppermute x14, waiting for transfers between devices, body(): arrived.append(lax.ppermute(blocks[slot], ('tcol', 'trow'), pair))  15.5 us
    unnamed x58, local copies, waits for them, and re-layouts  13.4 us
    all_to_all x1, starting transfers between devices, body(): lax.all_to_all(spectrum.reshape(freqs, 2 * points, src_rows), 'freq', spl...  11.4 us
    all_to_all x2, starting transfers between devices, body(): lax.all_to_all(replies.reshape(freqs, 2 * points, src_rows), 'freq', spli...  9.47 us
    pallas_call x4, Pallas kernels, reply_call(): pl.pallas_call(functools.partial(reply_kernel, sign, points, first, len(s...  6.29 us
  transfers between devices with their start and end apart: 17, of which 12 were waited for; matrix products, arithmetic and copies ran while one was open for 0% of the time, Pallas kernels for 11%

profile of v3, /device:TPU:32, one launch (start us, length us, event | category | flops | bytes accessed | tf_op | source)
XLA Modules:
  0.0 144.3 jit_solution(4562473669519696666)
XLA Ops:
  0.7 2.9 %dft_first.1 = bf16[256,768]{1,0:T(8,128)(2,1)} custom-call(bf16[256,256]{1,0:T(8,128)(2,1)} %constant.50.table_ref.table_hbm, s32[4,768]{1,0:T(4,128)} %window_ref.3, bf16[4,768,256]{2,1,0:T(8,128)(2,1)} %field_hbm.1), custom_call_target="tpu_custom_call" | custom-call | tf_op jit(solution)/shard_map/dft_first/pallas_call | solution.py:332
  3.5 11.4 %all-to-all-start = ((bf16[32,8,768]{2,1,0:T(8,128)(2,1)}), bf16[32,8,768]{2,1,0:T(8,128)(2,1)S(1)}, u32[]{:S(2)}, u32[]{:S(2)}) async-start(bf16[32,8,768]{2,1,0:T(8,128)(2,1)} %bitcast.20), calls=%async_computation | async-start | bytes 786432 | tf_op jit(solution)/shard_map/all_to_all | solution.py:384
  15.0 2.3 %copy-done.4 = bf16[1,16,2,96,2,384]{5,4,3,2,1,0:T(2,128)(2,1)S(1)} copy-done((bf16[1,16,2,96,2,384]{5,4,3,2,1,0:T(2,128)(2,1)S(1)}, bf16[1,16,2,96,2,384]{5,4,3,2,1,0:T(2,128)(2,1)}, u32[]{:S(2)}) %copy-start.4) | copy-done | bytes 4718616
  17.4 5.6 %prep_right.1 = (bf16[2,960,768]{2,1,0:T(8,128)(2,1)S(1)}, bf16[2,576,768]{2,1,0:T(8,128)(2,1)S(1)}) custom-call(s32[8]{0:T(128)S(1)} %fusion.2.place_ref, s32[16,2]{1,0:T(8,128)S(1)} %copy.12.rank_ref, bf16[1,16,2,96,2,384]{5,4,3,2,1,0:T(2,128)(2,1)S(1)} %copy-done.4), custom_call_target="tpu_custom_call" | custom-call | bytes 14155776 | tf_op jit(solution)/shard_map/prep_right/pallas_call | solution.py:323
  24.2 5.6 %all-to-all-done = bf16[32,8,768]{2,1,0:T(8,128)(2,1)S(1)} async-done(((bf16[32,8,768]{2,1,0:T(8,128)(2,1)}), bf16[32,8,768]{2,1,0:T(8,128)(2,1)S(1)}, u32[]{:S(2)}, u32[]{:S(2)}) %all-to-all-start) | async-done | bytes 393248 | tf_op jit(solution)/shard_map/all_to_all | solution.py:384
  36.2 2.0 %collective-permute-start.3 = (bf16[2,192,256]{2,1,0:T(8,128)(2,1)S(1)}, bf16[2,192,256]{2,1,0:T(8,128)(2,1)S(1)}, u32[]{:S(2)}, u32[]{:S(2)}) collective-permute-start(bf16[2,192,256]{2,1,0:T(8,128)(2,1)S(1)} %get-tuple-element.32), channel_id=1, source_target_pairs={{0,1},{1,0},{2,3},{3,2},{4,5},{5,4},{6,7},{7,6},{8,9},{9,8},{10,11... | collective-permute-start | bytes 589832 | tf_op jit(solution)/shard_map/ppermute | solution.py:430
  38.7 2.1 %collective-permute-start.4 = (bf16[2,192,256]{2,1,0:T(8,128)(2,1)S(1)}, bf16[2,192,256]{2,1,0:T(8,128)(2,1)S(1)}, u32[]{:S(2)}, u32[]{:S(2)}) collective-permute-start(bf16[2,192,256]{2,1,0:T(8,128)(2,1)S(1)} %coef.8), channel_id=1, source_target_pairs={{0,4},{1,5},{2,6},{3,7},{4,0},{5,1},{6,2},{7,3},{8,12},{9,13},{10,... | collective-permute-start | bytes 589832 | tf_op jit(solution)/shard_map/ppermute | solution.py:430
  41.9 3.8 %collective-permute-done.6.refs_4_ = bf16[2,192,256]{2,1,0:T(8,128)(2,1)} collective-permute-done((bf16[2,192,256]{2,1,0:T(8,128)(2,1)}, bf16[2,192,256]{2,1,0:T(8,128)(2,1)}, u32[]{:S(2)}, u32[]{:S(2)}) %collective-permute-start.6) | collective-permute-done | bytes 196640 | tf_op jit(solution)/shard_map/ppermute | solution.py:430
  46.1 3.1 %prep_left.1.refs_5_.refs_3_ = bf16[2,1536,768]{2,1,0:T(8,128)(2,1)S(1)} custom-call(s32[8]{0:T(128)S(1)} %fusion.5.place_ref, bf16[1,2,16,96,2,384]{5,4,3,2,1,0:T(2,128)(2,1)S(1)} %copy-done.5), custom_call_target="tpu_custom_call" | custom-call | bytes 14155776 | tf_op jit(solution)/shard_map/prep_left/pallas_call | solution.py:389
  50.1 2.1 %reply.4.refs_4_ = f32[2,256,768]{2,1,0:T(8,128)S(1)} custom-call(bf16[2,192,256]{2,1,0:T(8,128)(2,1)S(1)} %get-tuple-element.31.refs_0_, bf16[2,192,256]{2,1,0:T(8,128)(2,1)S(1)} %collective-permute-done.3.refs_1_, bf16[2,192,256]{2,1,0:T(8,128)(2,1)S(1)} %collective-permute-done.4.refs_2_, bf16[2,192,256]{2,1,0:T(8,128)(2,1)S(1)} %collective-permute-done.5.refs_3_, ...), custom_call_target="tpu_custom_call" | custom-call | flops 754974720 | bytes 2949120 | tf_op jit(solution)/shard_map/reply/pallas_call | solution.py:368
  52.3 1.8 %collective-permute-done.1.refs_1_ = bf16[2,192,256]{2,1,0:T(8,128)(2,1)S(1)} collective-permute-done((bf16[2,192,256]{2,1,0:T(8,128)(2,1)S(1)}, bf16[2,192,256]{2,1,0:T(8,128)(2,1)S(1)}, u32[]{:S(2)}, u32[]{:S(2)}) %collective-permute-start.1) | collective-permute-done | bytes 196640 | tf_op jit(solution)/shard_map/ppermute | solution.py:430
  54.6 1.6 %reply.5 = bf16[256,768]{1,0:T(8,128)(2,1)} custom-call(bf16[2,192,256]{2,1,0:T(8,128)(2,1)S(1)} %collective-permute-done.refs_0_, bf16[2,192,256]{2,1,0:T(8,128)(2,1)S(1)} %collective-permute-done.1.refs_1_, bf16[2,192,256]{2,1,0:T(8,128)(2,1)S(1)} %collective-permute-done.2.refs_2_, bf16[2,1536,768]{2,1,0:T(8,128)(2,1)S(1)} %prep_left.1.refs_5_.refs_3_, ...), custom_call_target="tpu_custom_call" | custom-call | flops 452984832 | bytes 1769472 | tf_op jit(solution)/shard_map/reply/pallas_call | solution.py:368
  56.2 4.8 %all-to-all-start.1 = ((bf16[32,8,768]{2,1,0:T(8,128)(2,1)}), bf16[32,8,768]{2,1,0:T(8,128)(2,1)S(1)}, u32[]{:S(2)}, u32[]{:S(2)}) async-start(bf16[32,8,768]{2,1,0:T(8,128)(2,1)} %bitcast.3), calls=%async_computation.1 | async-start | bytes 786432 | tf_op jit(solution)/shard_map/all_to_all | solution.py:435
  64.9 11.8 %all-to-all-done.1 = bf16[32,8,768]{2,1,0:T(8,128)(2,1)S(1)} async-done(((bf16[32,8,768]{2,1,0:T(8,128)(2,1)}), bf16[32,8,768]{2,1,0:T(8,128)(2,1)S(1)}, u32[]{:S(2)}, u32[]{:S(2)}) %all-to-all-start.1) | async-done | bytes 393248 | tf_op jit(solution)/shard_map/all_to_all | solution.py:435
  80.0 19.6 %all_to_all.20 = bf16[32,8,768]{2,1,0:T(8,128)(2,1)S(1)} all-to-all(bf16[32,8,768]{2,1,0:T(8,128)(2,1)S(1)} %bitcast.19), channel_id=1, replica_groups=mesh['freq'=32,'tcol'=4,'trow'=2] {'freq'}, dimensions={0} | all-to-all | bytes 786432 | tf_op jit(solution)/shard_map/all_to_all | solution.py:384
  104.0 2.9 %collective-permute-start.12 = (bf16[2,192,256]{2,1,0:T(8,128)(2,1)S(1)}, bf16[2,192,256]{2,1,0:T(8,128)(2,1)S(1)}, u32[]{:S(2)}, u32[]{:S(2)}) collective-permute-start(bf16[2,192,256]{2,1,0:T(8,128)(2,1)S(1)} %get-tuple-element.44), channel_id=1, source_target_pairs={{0,5},{1,4},{2,7},{3,6},{4,1},{5,0},{6,3},{7,2},{8,13},{9,12},{10,... | collective-permute-start | bytes 589832 | tf_op jit(solution)/shard_map/ppermute | solution.py:430
  107.2 2.3 %collective-permute-start.9 = (bf16[2,192,256]{2,1,0:T(8,128)(2,1)S(1)}, bf16[2,192,256]{2,1,0:T(8,128)(2,1)S(1)}, u32[]{:S(2)}, u32[]{:S(2)}) collective-permute-start(bf16[2,192,256]{2,1,0:T(8,128)(2,1)S(1)} %get-tuple-element.41), channel_id=1, source_target_pairs={{0,7},{1,6},{2,1},{3,0},{4,3},{5,2},{6,5},{7,4},{8,15},{9,14},{10,... | collective-permute-start | bytes 589832 | tf_op jit(solution)/shard_map/ppermute | solution.py:430
  109.5 1.5 %collective-permute-start.7 = (bf16[2,192,256]{2,1,0:T(8,128)(2,1)S(1)}, bf16[2,192,256]{2,1,0:T(8,128)(2,1)S(1)}, u32[]{:S(2)}, u32[]{:S(2)}) collective-permute-start(bf16[2,192,256]{2,1,0:T(8,128)(2,1)S(1)} %get-tuple-element.39), channel_id=1, source_target_pairs={{0,6},{1,7},{2,0},{3,1},{4,2},{5,3},{6,4},{7,5},{8,14},{9,15},{10,... | collective-permute-start | bytes 589832 | tf_op jit(solution)/shard_map/ppermute | solution.py:430
  112.2 4.8 %collective-permute-done.13.refs_4_ = bf16[2,192,256]{2,1,0:T(8,128)(2,1)S(1)} collective-permute-done((bf16[2,192,256]{2,1,0:T(8,128)(2,1)S(1)}, bf16[2,192,256]{2,1,0:T(8,128)(2,1)S(1)}, u32[]{:S(2)}, u32[]{:S(2)}) %collective-permute-start.13) | collective-permute-done | bytes 196640 | tf_op jit(solution)/shard_map/ppermute | solution.py:430
  118.1 2.7 %collective-permute-done.7.refs_0_ = bf16[2,192,256]{2,1,0:T(8,128)(2,1)S(1)} collective-permute-done((bf16[2,192,256]{2,1,0:T(8,128)(2,1)S(1)}, bf16[2,192,256]{2,1,0:T(8,128)(2,1)S(1)}, u32[]{:S(2)}, u32[]{:S(2)}) %collective-permute-start.7) | collective-permute-done | bytes 196640 | tf_op jit(solution)/shard_map/ppermute | solution.py:430
  121.1 1.6 %reply.7 = bf16[256,768]{1,0:T(8,128)(2,1)} custom-call(bf16[2,192,256]{2,1,0:T(8,128)(2,1)S(1)} %collective-permute-done.7.refs_0_, bf16[2,192,256]{2,1,0:T(8,128)(2,1)S(1)} %collective-permute-done.8.refs_1_, bf16[2,192,256]{2,1,0:T(8,128)(2,1)S(1)} %collective-permute-done.9.refs_2_, bf16[2,1536,768]{2,1,0:T(8,128)(2,1)S(1)} %bitcast.10, ...), custom_call_target="tpu_custom_call" | custom-call | flops 452984832 | bytes 1769472 | tf_op jit(solution)/shard_map/reply/pallas_call | solution.py:368
  122.7 4.7 %all-to-all-start.3 = ((bf16[32,8,768]{2,1,0:T(8,128)(2,1)}), bf16[32,8,768]{2,1,0:T(8,128)(2,1)S(1)}, u32[]{:S(2)}, u32[]{:S(2)}) async-start(bf16[32,8,768]{2,1,0:T(8,128)(2,1)} %bitcast.7), calls=%async_computation.3 | async-start | bytes 786432 | tf_op jit(solution)/shard_map/all_to_all | solution.py:435
  128.7 13.9 %all-to-all-done.3 = bf16[32,8,768]{2,1,0:T(8,128)(2,1)S(1)} async-done(((bf16[32,8,768]{2,1,0:T(8,128)(2,1)}), bf16[32,8,768]{2,1,0:T(8,128)(2,1)S(1)}, u32[]{:S(2)}, u32[]{:S(2)}) %all-to-all-start.3) | async-done | bytes 393248 | tf_op jit(solution)/shard_map/all_to_all | solution.py:435
  142.6 1.5 %last.1 = bf16[4,768,256]{2,1,0:T(8,128)(2,1)} custom-call(bf16[256,1024]{1,0:T(8,128)(2,1)S(1)} %copy-done.11, bf16[4,768,128]{2,1,0:T(8,128)(2,1)S(1)} %copy-done.9, bf16[256,768]{1,0:T(8,128)(2,1)S(1)} %bitcast.17), custom_call_target="tpu_custom_call" | custom-call | tf_op jit(solution)/shard_map/last/pallas_call | solution.py:449
  (90 shorter events, 26.7 us)
Async XLA Ops:
  0.6 14.4 %copy-start.25 = (s32[8]{0:T(128)S(1)}, s32[8]{0:T(128)}, u32[]{:S(2)}) copy-start(s32[8]{0:T(128)} %constant.41.clone) | copy-start | bytes 100
  0.6 14.4 %copy-start.26 = (s32[8]{0:T(128)S(1)}, s32[8]{0:T(128)}, u32[]{:S(2)}) copy-start(s32[8]{0:T(128)} %constant.42.clone) | copy-start | bytes 100
  3.5 26.3 %all-to-all-start = ((bf16[32,8,768]{2,1,0:T(8,128)(2,1)}), bf16[32,8,768]{2,1,0:T(8,128)(2,1)S(1)}, u32[]{:S(2)}, u32[]{:S(2)}) async-start(bf16[32,8,768]{2,1,0:T(8,128)(2,1)} %bitcast.20), calls=%async_computation | async-start | bytes 786432 | tf_op jit(solution)/shard_map/all_to_all | solution.py:384
  32.6 9.2 %collective-permute-start.5 = (bf16[2,192,256]{2,1,0:T(8,128)(2,1)}, bf16[2,192,256]{2,1,0:T(8,128)(2,1)S(1)}, u32[]{:S(2)}, u32[]{:S(2)}) collective-permute-start(bf16[2,192,256]{2,1,0:T(8,128)(2,1)} %get-tuple-element.33), channel_id=1, source_target_pairs={{0,5},{1,4},{2,7},{3,6},{4,1},{5,0},{6,3},{7,2},{8,13},{9,12},{10,... | collective-permute-start | bytes 589832 | tf_op jit(solution)/shard_map/ppermute | solution.py:430
  33.2 12.5 %collective-permute-start.6 = (bf16[2,192,256]{2,1,0:T(8,128)(2,1)}, bf16[2,192,256]{2,1,0:T(8,128)(2,1)}, u32[]{:S(2)}, u32[]{:S(2)}) collective-permute-start(bf16[2,192,256]{2,1,0:T(8,128)(2,1)} %get-tuple-element.34), channel_id=1, source_target_pairs={{0,2},{1,3},{2,4},{3,5},{4,6},{5,7},{6,0},{7,1},{8,10},{9,11},{10,... | collective-permute-start | bytes 589832 | tf_op jit(solution)/shard_map/ppermute | solution.py:430
  36.2 13.0 %collective-permute-start.3 = (bf16[2,192,256]{2,1,0:T(8,128)(2,1)S(1)}, bf16[2,192,256]{2,1,0:T(8,128)(2,1)S(1)}, u32[]{:S(2)}, u32[]{:S(2)}) collective-permute-start(bf16[2,192,256]{2,1,0:T(8,128)(2,1)S(1)} %get-tuple-element.32), channel_id=1, source_target_pairs={{0,1},{1,0},{2,3},{3,2},{4,5},{5,4},{6,7},{7,6},{8,9},{9,8},{10,11... | collective-permute-start | bytes 589832 | tf_op jit(solution)/shard_map/ppermute | solution.py:430
  38.7 11.4 %collective-permute-start.4 = (bf16[2,192,256]{2,1,0:T(8,128)(2,1)S(1)}, bf16[2,192,256]{2,1,0:T(8,128)(2,1)S(1)}, u32[]{:S(2)}, u32[]{:S(2)}) collective-permute-start(bf16[2,192,256]{2,1,0:T(8,128)(2,1)S(1)} %coef.8), channel_id=1, source_target_pairs={{0,4},{1,5},{2,6},{3,7},{4,0},{5,1},{6,2},{7,3},{8,12},{9,13},{10,... | collective-permute-start | bytes 589832 | tf_op jit(solution)/shard_map/ppermute | solution.py:430
  40.8 11.5 %collective-permute-start = (bf16[2,192,256]{2,1,0:T(8,128)(2,1)S(1)}, bf16[2,192,256]{2,1,0:T(8,128)(2,1)S(1)}, u32[]{:S(2)}, u32[]{:S(2)}) collective-permute-start(bf16[2,192,256]{2,1,0:T(8,128)(2,1)S(1)} %copy-done.21), channel_id=1, source_target_pairs={{0,6},{1,7},{2,0},{3,1},{4,2},{5,3},{6,4},{7,5},{8,14},{9,15},{10,... | collective-permute-start | bytes 589832 | tf_op jit(solution)/shard_map/ppermute | solution.py:430
  41.8 12.4 %collective-permute-start.1 = (bf16[2,192,256]{2,1,0:T(8,128)(2,1)S(1)}, bf16[2,192,256]{2,1,0:T(8,128)(2,1)S(1)}, u32[]{:S(2)}, u32[]{:S(2)}) collective-permute-start(bf16[2,192,256]{2,1,0:T(8,128)(2,1)S(1)} %copy-done.19), channel_id=1, source_target_pairs={{0,3},{1,2},{2,5},{3,4},{4,7},{5,6},{6,1},{7,0},{8,11},{9,10},{10,... | collective-permute-start | bytes 589832 | tf_op jit(solution)/shard_map/ppermute | solution.py:430
  45.7 8.9 %collective-permute-start.2 = (bf16[2,192,256]{2,1,0:T(8,128)(2,1)S(1)}, bf16[2,192,256]{2,1,0:T(8,128)(2,1)S(1)}, u32[]{:S(2)}, u32[]{:S(2)}) collective-permute-start(bf16[2,192,256]{2,1,0:T(8,128)(2,1)S(1)} %get-tuple-element.30), channel_id=1, source_target_pairs={{0,7},{1,6},{2,1},{3,0},{4,3},{5,2},{6,5},{7,4},{8,15},{9,14},{10,... | collective-permute-start | bytes 589832 | tf_op jit(solution)/shard_map/ppermute | solution.py:430
  56.2 20.5 %all-to-all-start.1 = ((bf16[32,8,768]{2,1,0:T(8,128)(2,1)}), bf16[32,8,768]{2,1,0:T(8,128)(2,1)S(1)}, u32[]{:S(2)}, u32[]{:S(2)}) async-start(bf16[32,8,768]{2,1,0:T(8,128)(2,1)} %bitcast.3), calls=%async_computation.1 | async-start | bytes 786432 | tf_op jit(solution)/shard_map/all_to_all | solution.py:435
  78.8 38.3 %slice-start = ((s8[4718592]{0:T(1024)(128)(4,1)}), s8[4194304]{0:T(1024)(128)(4,1)S(1)}, s32[]{:S(2)}) async-start(s8[4718592]{0:T(1024)(128)(4,1)} %bitcast.9), calls=%async_computation.4 | async-start | bytes 8388608
  79.9 20.1 %copy-start.6 = (bf16[4,256,768]{2,1,0:T(8,128)(2,1)}, bf16[4,256,768]{2,1,0:T(8,128)(2,1)S(1)}, u32[]{:S(2)}) copy-start(bf16[4,256,768]{2,1,0:T(8,128)(2,1)S(1)} %get-tuple-element.35.turned_ref) | copy-start | bytes 4718596
  99.6 17.5 %slice-start.1 = ((s8[4718592]{0:T(1024)(128)(4,1)}), s8[524288]{0:T(1024)(128)(4,1)S(1)}, s32[]{:S(2)}) async-start(s8[4718592]{0:T(1024)(128)(4,1)} %bitcast.9), calls=%async_computation.5 | async-start | bytes 1048576
  100.0 9.4 %collective-permute-start.11 = (bf16[2,192,256]{2,1,0:T(8,128)(2,1)S(1)}, bf16[2,192,256]{2,1,0:T(8,128)(2,1)S(1)}, u32[]{:S(2)}, u32[]{:S(2)}) collective-permute-start(bf16[2,192,256]{2,1,0:T(8,128)(2,1)S(1)} %coef.11), channel_id=1, source_target_pairs={{0,4},{1,5},{2,6},{3,7},{4,0},{5,1},{6,2},{7,3},{8,12},{9,13},{10,... | collective-permute-start | bytes 589832 | tf_op jit(solution)/shard_map/ppermute | solution.py:430
  103.1 7.9 %collective-permute-start.10 = (bf16[2,192,256]{2,1,0:T(8,128)(2,1)S(1)}, bf16[2,192,256]{2,1,0:T(8,128)(2,1)S(1)}, u32[]{:S(2)}, u32[]{:S(2)}) collective-permute-start(bf16[2,192,256]{2,1,0:T(8,128)(2,1)S(1)} %get-tuple-element.43), channel_id=1, source_target_pairs={{0,1},{1,0},{2,3},{3,2},{4,5},{5,4},{6,7},{7,6},{8,9},{9,8},{10,11... | collective-permute-start | bytes 589832 | tf_op jit(solution)/shard_map/ppermute | solution.py:430
  104.0 8.3 %collective-permute-start.12 = (bf16[2,192,256]{2,1,0:T(8,128)(2,1)S(1)}, bf16[2,192,256]{2,1,0:T(8,128)(2,1)S(1)}, u32[]{:S(2)}, u32[]{:S(2)}) collective-permute-start(bf16[2,192,256]{2,1,0:T(8,128)(2,1)S(1)} %get-tuple-element.44), channel_id=1, source_target_pairs={{0,5},{1,4},{2,7},{3,6},{4,1},{5,0},{6,3},{7,2},{8,13},{9,12},{10,... | collective-permute-start | bytes 589832 | tf_op jit(solution)/shard_map/ppermute | solution.py:430
  106.9 10.2 %collective-permute-start.13 = (bf16[2,192,256]{2,1,0:T(8,128)(2,1)S(1)}, bf16[2,192,256]{2,1,0:T(8,128)(2,1)S(1)}, u32[]{:S(2)}, u32[]{:S(2)}) collective-permute-start(bf16[2,192,256]{2,1,0:T(8,128)(2,1)S(1)} %get-tuple-element.45), channel_id=1, source_target_pairs={{0,2},{1,3},{2,4},{3,5},{4,6},{5,7},{6,0},{7,1},{8,10},{9,11},{10,... | collective-permute-start | bytes 589832 | tf_op jit(solution)/shard_map/ppermute | solution.py:430
  107.2 10.9 %collective-permute-start.9 = (bf16[2,192,256]{2,1,0:T(8,128)(2,1)S(1)}, bf16[2,192,256]{2,1,0:T(8,128)(2,1)S(1)}, u32[]{:S(2)}, u32[]{:S(2)}) collective-permute-start(bf16[2,192,256]{2,1,0:T(8,128)(2,1)S(1)} %get-tuple-element.41), channel_id=1, source_target_pairs={{0,7},{1,6},{2,1},{3,0},{4,3},{5,2},{6,5},{7,4},{8,15},{9,14},{10,... | collective-permute-start | bytes 589832 | tf_op jit(solution)/shard_map/ppermute | solution.py:430
  109.5 11.4 %collective-permute-start.7 = (bf16[2,192,256]{2,1,0:T(8,128)(2,1)S(1)}, bf16[2,192,256]{2,1,0:T(8,128)(2,1)S(1)}, u32[]{:S(2)}, u32[]{:S(2)}) collective-permute-start(bf16[2,192,256]{2,1,0:T(8,128)(2,1)S(1)} %get-tuple-element.39), channel_id=1, source_target_pairs={{0,6},{1,7},{2,0},{3,1},{4,2},{5,3},{6,4},{7,5},{8,14},{9,15},{10,... | collective-permute-start | bytes 589832 | tf_op jit(solution)/shard_map/ppermute | solution.py:430
  111.0 10.1 %collective-permute-start.8 = (bf16[2,192,256]{2,1,0:T(8,128)(2,1)S(1)}, bf16[2,192,256]{2,1,0:T(8,128)(2,1)S(1)}, u32[]{:S(2)}, u32[]{:S(2)}) collective-permute-start(bf16[2,192,256]{2,1,0:T(8,128)(2,1)S(1)} %get-tuple-element.40), channel_id=1, source_target_pairs={{0,3},{1,2},{2,5},{3,4},{4,7},{5,6},{6,1},{7,0},{8,11},{9,10},{10,... | collective-permute-start | bytes 589832 | tf_op jit(solution)/shard_map/ppermute | solution.py:430
  122.7 20.0 %all-to-all-start.3 = ((bf16[32,8,768]{2,1,0:T(8,128)(2,1)}), bf16[32,8,768]{2,1,0:T(8,128)(2,1)S(1)}, u32[]{:S(2)}, u32[]{:S(2)}) async-start(bf16[32,8,768]{2,1,0:T(8,128)(2,1)} %bitcast.7), calls=%async_computation.3 | async-start | bytes 786432 | tf_op jit(solution)/shard_map/all_to_all | solution.py:435
  127.4 15.3 %copy-start.9 = (bf16[4,768,128]{2,1,0:T(8,128)(2,1)S(1)}, bf16[4,768,128]{2,1,0:T(8,128)(2,1)}, u32[]{:S(2)}) copy-start(bf16[4,768,128]{2,1,0:T(8,128)(2,1)} %copy-done.8) | copy-start | bytes 2359300
  127.4 15.3 %copy-start.11 = (bf16[256,1024]{1,0:T(8,128)(2,1)S(1)}, bf16[256,1024]{1,0:T(8,128)(2,1)}, u32[]{:S(2)}) copy-start(bf16[256,1024]{1,0:T(8,128)(2,1)} %copy-done.10) | copy-start | bytes 1572868
  (22 other events, 97.2 us)
